TPU v7x, 32 devices: a whole 2x2x4 slice. The times are simulated.
32 devices in a mesh: section: 4 (over z), seq: 8 (over y, x, core).
Axes of the slice: x: 2, y: 2, z: 4, core: 2. Of those that a mesh axis runs over, the one named last changes fastest.
Arguments:
- x_a: bfloat16 [1024, 4096], P('seq'), may hold values from -6 to 6
- x_b: bfloat16 [1024, 4096], P('seq'), may hold values from -6 to 6
- grad_a: bfloat16 [1024, 4096], P('seq'), may hold values from -6 to 6
- grad_b: bfloat16 [1024, 4096], P('seq'), may hold values from -6 to 6
- gains: float32 [4, 2, 4096], P('section'), may hold values from 0.5 to 1.5
- kv_weights: bfloat16 [4, 2, 4096, 1024], P('section'), may hold values from -0.09375 to 0.09375
- doc_lengths: int32 [2, 16], replicated, may hold values from 1 to 128, 1024 in all within a row
Outputs:
- acts: bfloat16 [2, 4, 1024, 4096], P(None, 'section', 'seq')
- in_grads: bfloat16 [2, 4, 1024, 4096], P(None, 'section', 'seq')
- kv_grads: bfloat16 [2, 4, 1024, 1024], P(None, 'section', 'seq')
Inputs may be any that keep to these rules, and one draw needn't show every extreme that they name: `doc_lengths`: each row lists 16 documents that fill the 1024 tokens of its sequence in order; in each row some document is exactly 128 tokens long.
All inputs are finite; a program needn't handle non-finite values.
Results may differ from a plain program's by a relative error of at most 0.024.
Values may be sent and summed in bfloat16 or wider, within the bound.
A program may use at most 320 MiB of HBM per device.

v0:
```python
import functools
import math

import jax
import jax.numpy as jnp
from jax import lax
from jax.experimental import pallas as pl
from jax.experimental.pallas import tpu as pltpu
from jax.sharding import PartitionSpec as P

HEADS = 32
HEAD_DIM = 128
KV_HEADS = 4
REACH = 1
GROUP = HEADS // KV_HEADS
SCALE = 1.0 / math.sqrt(HEAD_DIM)

epsilon = 1e-05

F32 = jnp.float32
BF16 = jnp.bfloat16


def passed_along(block, axis, distance):
    devices = range(lax.axis_size(axis))
    route = [(i - distance, i) for i in devices if i - distance in devices]
    return lax.ppermute(block, axis, route)


def dot(a, b, dims):
    return lax.dot_general(a, b, (dims, ((), ())), preferred_element_type=F32)


def project_kernel(slot_ref, h_ref, gain_ref, weight_ref, pairs_ref, normed_ref):
    @pl.when(pl.program_id(0) == 0)
    def _():
        widened = h_ref[...].astype(F32)
        square_mean = jnp.mean(widened * widened, axis=-1, keepdims=True)
        normed_ref[...] = (widened * lax.rsqrt(square_mean + epsilon) * gain_ref[0]).astype(BF16)

    pairs_ref[...] = dot(normed_ref[...], weight_ref[0], ((1,), (0,))).astype(BF16)


def project(slot, stream, gains, weights):
    rows, width = stream.shape
    pair_width = weights.shape[-1]
    tile = pair_width // 4
    return pl.pallas_call(
        project_kernel,
        grid_spec=pltpu.PrefetchScalarGridSpec(
            num_scalar_prefetch=1,
            grid=(pair_width // tile,),
            in_specs=[
                pl.BlockSpec((rows, width), lambda j, s: (0, 0)),
                pl.BlockSpec((1, 1, width), lambda j, s: (s[0], 0, 0)),
                pl.BlockSpec((1, width, tile), lambda j, s: (s[0], 0, j)),
            ],
            out_specs=[
                pl.BlockSpec((rows, tile), lambda j, s: (0, j)),
                pl.BlockSpec((rows, width), lambda j, s: (0, 0)),
            ],
        ),
        out_shape=[
            jax.ShapeDtypeStruct((rows, pair_width), BF16),
            jax.ShapeDtypeStruct((rows, width), BF16),
        ],
        cost_estimate=pl.CostEstimate(
            flops=2 * rows * width * pair_width,
            bytes_accessed=2 * width * pair_width,
            transcendentals=0,
        ),
        name="project",
    )(slot, stream, gains, weights)


def softmax_parts(query, keys, mask):
    scores = dot(query, keys, ((1,), (1,))) * SCALE
    scores = jnp.where(mask, scores, -1e30)
    powers = jnp.exp(scores - jnp.max(scores, axis=-1, keepdims=True))
    return powers * (1.0 / jnp.sum(powers, axis=-1, keepdims=True))


def mix_kernel(h_ref, normed_ref, kp_ref, ko_ref, vp_ref, vo_ref, mask_ref, out_ref):
    keys = jnp.concatenate([kp_ref[...], ko_ref[...]], axis=0)
    values = jnp.concatenate([vp_ref[...], vo_ref[...]], axis=0)
    mask = mask_ref[...] > 0.0
    for head in range(GROUP):
        cols = slice(head * HEAD_DIM, (head + 1) * HEAD_DIM)
        weights = softmax_parts(normed_ref[:, cols], keys, mask).astype(BF16)
        mixture = dot(weights, values, ((1,), (0,)))
        out_ref[:, cols] = (h_ref[:, cols].astype(F32) + mixture).astype(BF16)


def head_specs(rows):
    return [
        pl.BlockSpec((rows, HEAD_DIM), lambda k: (0, k)),
        pl.BlockSpec((rows, HEAD_DIM), lambda k: (0, k)),
        pl.BlockSpec((rows, HEAD_DIM), lambda k: (0, KV_HEADS + k)),
        pl.BlockSpec((rows, HEAD_DIM), lambda k: (0, KV_HEADS + k)),
    ]


def mix(stream, normed, earlier, own, mask):
    rows, width = stream.shape
    block = pl.BlockSpec((rows, GROUP * HEAD_DIM), lambda k: (0, k))
    return pl.pallas_call(
        mix_kernel,
        grid=(KV_HEADS,),
        in_specs=[block, block] + head_specs(rows) + [pl.BlockSpec(mask.shape, lambda k: (0, 0))],
        out_specs=block,
        out_shape=jax.ShapeDtypeStruct((rows, width), BF16),
        cost_estimate=pl.CostEstimate(
            flops=8 * rows * rows * width, bytes_accessed=6 * rows * width, transcendentals=0
        ),
        name="mix",
    )(stream, normed, earlier, own, earlier, own, mask)


def reverse_kernel(
    c_ref, normed_ref, kp_ref, ko_ref, vp_ref, vo_ref, mask_ref,
    dq_ref, dkp_ref, dko_ref, dvp_ref, dvo_ref,
):
    rows = c_ref.shape[0]
    keys = jnp.concatenate([kp_ref[...], ko_ref[...]], axis=0)
    values = jnp.concatenate([vp_ref[...], vo_ref[...]], axis=0)
    mask = mask_ref[...] > 0.0
    weight_list, score_list, query_list, cot_list = [], [], [], []
    for head in range(GROUP):
        cols = slice(head * HEAD_DIM, (head + 1) * HEAD_DIM)
        query = normed_ref[:, cols]
        cot = c_ref[:, cols]
        weights = softmax_parts(query, keys, mask)
        grad_w = dot(cot, values, ((1,), (1,)))
        inner = jnp.sum(grad_w * weights, axis=-1, keepdims=True)
        grad_s = (weights * (grad_w - inner) * SCALE).astype(BF16)
        dq_ref[:, cols] = dot(grad_s, keys, ((1,), (0,))).astype(BF16)
        weight_list.append(weights.astype(BF16))
        score_list.append(grad_s)
        query_list.append(query)
        cot_list.append(cot)
    all_s = jnp.concatenate(score_list, axis=0)
    all_w = jnp.concatenate(weight_list, axis=0)
    all_q = jnp.concatenate(query_list, axis=0)
    all_c = jnp.concatenate(cot_list, axis=0)
    grad_k = dot(all_s, all_q, ((0,), (0,))).astype(BF16)
    grad_v = dot(all_w, all_c, ((0,), (0,))).astype(BF16)
    dkp_ref[...] = grad_k[:rows]
    dko_ref[...] = grad_k[rows:]
    dvp_ref[...] = grad_v[:rows]
    dvo_ref[...] = grad_v[rows:]


def reverse_mix(cotangent, normed, earlier, own, mask):
    rows, width = cotangent.shape
    block = pl.BlockSpec((rows, GROUP * HEAD_DIM), lambda k: (0, k))
    half = pl.BlockSpec((rows, HEAD_DIM), lambda k: (0, k))
    half_shape = jax.ShapeDtypeStruct((rows, KV_HEADS * HEAD_DIM), BF16)
    return pl.pallas_call(
        reverse_kernel,
        grid=(KV_HEADS,),
        in_specs=[block, block] + head_specs(rows) + [pl.BlockSpec(mask.shape, lambda k: (0, 0))],
        out_specs=[block, half, half, half, half],
        out_shape=[jax.ShapeDtypeStruct((rows, width), BF16)] + [half_shape] * 4,
        cost_estimate=pl.CostEstimate(
            flops=20 * rows * rows * width, bytes_accessed=6 * rows * width, transcendentals=0
        ),
        name="reverse_mix",
    )(cotangent, normed, earlier, own, earlier, own, mask)


def reverse_project_kernel(
    steps, slot_ref, c_ref, dq_ref, h_ref, gain_ref, dk_ref, rk_ref, dv_ref, rv_ref, weight_ref,
    total_ref, pairs_ref, grad_scr,
):
    step = pl.program_id(0)
    tile = weight_ref.shape[1]

    @pl.when(step == 0)
    def _():
        half = dk_ref.shape[1]
        pairs_ref[:, :half] = (dk_ref[...].astype(F32) + rk_ref[...].astype(F32)).astype(BF16)
        pairs_ref[:, half:] = (dv_ref[...].astype(F32) + rv_ref[...].astype(F32)).astype(BF16)

    grad_scr[step] = dot(pairs_ref[...], weight_ref[0], ((1,), (1,))).astype(BF16)

    @pl.when(step == steps - 1)
    def _():
        widened = h_ref[...].astype(F32)
        width = widened.shape[1]
        rstd = lax.rsqrt(jnp.mean(widened * widened, axis=-1, keepdims=True) + epsilon)
        inner = jnp.zeros_like(rstd)
        for j in range(steps):
            cols = slice(j * tile, (j + 1) * tile)
            grad_n = (grad_scr[j].astype(F32) + dq_ref[:, cols].astype(F32)) * gain_ref[0, :, cols]
            inner = inner + jnp.sum(grad_n * widened[:, cols], axis=-1, keepdims=True)
        factor = inner * (1.0 / width) * rstd * rstd * rstd
        for j in range(steps):
            cols = slice(j * tile, (j + 1) * tile)
            grad_n = (grad_scr[j].astype(F32) + dq_ref[:, cols].astype(F32)) * gain_ref[0, :, cols]
            grad_h = grad_n * rstd - widened[:, cols] * factor
            total_ref[:, cols] = (c_ref[:, cols].astype(F32) + grad_h).astype(BF16)


def reverse_project(slot, cotangent, grad_q, stream, gains, grads, weights):
    rows, width = stream.shape
    pair_width = weights.shape[-1]
    steps = 4
    tile = width // steps
    full = pl.BlockSpec((rows, width), lambda j, s: (0, 0))
    half = pl.BlockSpec((rows, pair_width // 2), lambda j, s: (0, 0))
    return pl.pallas_call(
        functools.partial(reverse_project_kernel, steps),
        grid_spec=pltpu.PrefetchScalarGridSpec(
            num_scalar_prefetch=1,
            grid=(steps,),
            in_specs=[full, full, full, pl.BlockSpec((1, 1, width), lambda j, s: (s[0], 0, 0))]
            + [half] * 4
            + [pl.BlockSpec((1, tile, pair_width), lambda j, s: (s[0], j, 0))],
            out_specs=[full, pl.BlockSpec((rows, pair_width), lambda j, s: (0, 0))],
            scratch_shapes=[pltpu.VMEM((steps, rows, tile), BF16)],
        ),
        out_shape=[
            jax.ShapeDtypeStruct((rows, width), BF16),
            jax.ShapeDtypeStruct((rows, pair_width), BF16),
        ],
        cost_estimate=pl.CostEstimate(
            flops=2 * rows * width * pair_width,
            bytes_accessed=2 * width * pair_width,
            transcendentals=0,
        ),
        name="reverse_project",
    )(slot, cotangent, grad_q, stream, gains, *grads, weights)


def per_device(x_a, x_b, grad_a, grad_b, gains, kv_weights, doc_lengths):
    count = lax.axis_size("section")
    section = lax.axis_index("section")
    shard = lax.axis_index("seq")
    rows = x_a.shape[0]
    places = shard * rows + jnp.arange(rows, dtype=jnp.int32)
    key_places = (shard - REACH) * rows + jnp.arange((REACH + 1) * rows, dtype=jnp.int32)
    ends = jnp.cumsum(doc_lengths, axis=1)

    def mask_of(direction):
        docs_q = jnp.sum((ends[direction][None, :] <= places[:, None]).astype(jnp.int32), axis=1)
        docs_k = jnp.sum((ends[direction][None, :] <= key_places[:, None]).astype(jnp.int32), axis=1)
        allowed = (
            (docs_q[:, None] == docs_k[None, :])
            & (key_places[None, :] <= places[:, None])
            & (key_places[None, :] >= 0)
        )
        return allowed.astype(F32)

    mask_down, mask_up = mask_of(0), mask_of(1)
    gain_pair = gains[0][:, None, :]
    weight_pair = kv_weights[0]

    saved = {}
    held_down, held_up = x_a, x_b
    for step in range(count):
        down = section == step
        up = section == count - 1 - step
        slot = jnp.where(down, 0, 1).astype(jnp.int32)[None]
        stream = jnp.where(down, held_down, held_up)
        mask = jnp.where(down, mask_down, mask_up)
        own, normed = project(slot, stream, gain_pair, weight_pair)
        earlier = passed_along(own, "seq", REACH)
        output = mix(stream, normed, earlier, own, mask)
        if step + 1 < count:
            held_down = passed_along(output, "section", 1)
            held_up = passed_along(output, "section", -1)
        fresh = (stream, normed, own, earlier, output)
        for name, chosen in (("down", down), ("up", up)):
            before = saved.get(name)
            saved[name] = (
                fresh
                if before is None
                else tuple(jnp.where(chosen, new, old) for new, old in zip(fresh, before))
            )
    acts_out = jnp.stack([saved["down"][4], saved["up"][4]])[:, None]

    held_down, held_up = grad_a, grad_b
    results = {}
    for step in range(count):
        down = section == count - 1 - step
        up = section == step
        slot = jnp.where(down, 0, 1).astype(jnp.int32)[None]
        cotangent = jnp.where(down, held_down, held_up)
        stream, normed, own, earlier = (
            jnp.where(down, a, b) for a, b in zip(saved["down"][:4], saved["up"][:4])
        )
        mask = jnp.where(down, mask_down, mask_up)
        grad_q, dkp, dko, dvp, dvo = reverse_mix(cotangent, normed, earlier, own, mask)
        rk = passed_along(dkp, "seq", 0 - REACH)
        rv = passed_along(dvp, "seq", 0 - REACH)
        total, pairs = reverse_project(
            slot, cotangent, grad_q, stream, gain_pair, (dko, rk, dvo, rv), weight_pair
        )
        if step + 1 < count:
            held_down = passed_along(total, "section", -1)
            held_up = passed_along(total, "section", 1)
        fresh = (total, pairs)
        for name, chosen in (("down", down), ("up", up)):
            before = results.get(name)
            results[name] = (
                fresh
                if before is None
                else tuple(jnp.where(chosen, new, old) for new, old in zip(fresh, before))
            )
    ingrad_out = jnp.stack([results["down"][0], results["up"][0]])[:, None]
    kvgrad_out = jnp.stack([results["down"][1], results["up"][1]])[:, None]
    return (acts_out, ingrad_out, kvgrad_out)


def solution(mesh):
    in_specs = (
        P("seq", None),
        P("seq", None),
        P("seq", None),
        P("seq", None),
        P("section", None, None),
        P("section", None, None, None),
        P(),
    )
    out_specs = (
        P(None, "section", "seq", None),
        P(None, "section", "seq", None),
        P(None, "section", "seq", None),
    )
    return jax.shard_map(
        per_device, mesh=mesh, in_specs=in_specs, out_specs=out_specs, check_vma=False
    )
```

profile of v0, /device:TPU:1, one launch (start us, length us, event | category | flops | bytes accessed | tf_op | source)
XLA Modules:
  0.0 396.3 jit_solution(16161628530833109399)
XLA Ops:
  2.0 2.3 broadcast_select_fusion.3.h_ref
  4.3 6.4 %project.4 = (bf16[128,1024]{1,0:T(8,128)(2,1)}, bf16[128,4096]{1,0:T(8,128)(2,1)}) custom-call(s32[1]{0:T(128)} %bitcast.slot_ref, bf16[128,4096]{1,0:T(8,128)(2,1)} %broadcast_select_fusion.3.h_ref, f32[2,1,4096]{2,1,0:T(1,128)} %broadcast_in_dim_squeeze.3.gain_ref, bf16[2,4096,1024]{2,1,0:T(8,128)(2,1)} %bitcast.33), custom_call_target="tpu_custom_call" | custom-call | flops 1073741824 | bytes 8388608 | tf_op jit(solution)/shard_map/project/pallas_call | solution.py:48
  10.8 4.5 %collective-permute-start = (bf16[128,1024]{1,0:T(8,128)(2,1)}, bf16[128,1024]{1,0:T(8,128)(2,1)S(1)}, u32[]{:S(2)}, u32[]{:S(2)}) collective-permute-start(bf16[128,1024]{1,0:T(8,128)(2,1)} %get-tuple-element.40.ko_ref.vo_ref), channel_id=1, source_target_pairs={{0,1},{1,2},{2,3},{3,4},{4,5},{5,6},{6,7},{8,9},{9,10},{10,11},{11... | collective-permute-start | bytes 786440 | tf_op jit(solution)/shard_map/ppermute | solution.py:27
  16.6 2.2 collective-permute-done.kp_ref.vp_ref
  19.6 6.5 %mix.4 = bf16[128,4096]{1,0:T(8,128)(2,1)} custom-call(bf16[128,4096]{1,0:T(8,128)(2,1)} %broadcast_select_fusion.3.h_ref, bf16[128,4096]{1,0:T(8,128)(2,1)} %get-tuple-element.39.normed_ref, bf16[128,1024]{1,0:T(8,128)(2,1)} %copy-done.18, bf16[128,1024]{1,0:T(8,128)(2,1)} %get-tuple-element.40.ko_ref.vo_ref, bf16[128,1024]{1,0:T(8,128)(2,1)} %copy-done.18, ...), custom_call_target="tpu_custom_call" | custom-call | flops 536870912 | bytes 3145728 | tf_op jit(solution)/shard_map/mix/pallas_call | solution.py:106
  26.1 3.2 collective-permute-start.1
  30.6 18.9 %collective-permute-done.1 = bf16[128,4096]{1,0:T(8,128)(2,1)S(1)} collective-permute-done((bf16[128,4096]{1,0:T(8,128)(2,1)}, bf16[128,4096]{1,0:T(8,128)(2,1)S(1)}, u32[]{:S(2)}, u32[]{:S(2)}) %collective-permute-start.1) | collective-permute-done | bytes 1048608 | tf_op jit(solution)/shard_map/ppermute | solution.py:27
  49.5 4.1 %collective-permute-done.2 = bf16[128,4096]{1,0:T(8,128)(2,1)S(1)} collective-permute-done((bf16[128,4096]{1,0:T(8,128)(2,1)}, bf16[128,4096]{1,0:T(8,128)(2,1)S(1)}, u32[]{:S(2)}, u32[]{:S(2)}) %collective-permute-start.2) | collective-permute-done | bytes 1048608 | tf_op jit(solution)/shard_map/ppermute | solution.py:27
  54.6 6.5 %project.5 = (bf16[128,1024]{1,0:T(8,128)(2,1)}, bf16[128,4096]{1,0:T(8,128)(2,1)}) custom-call(s32[1]{0:T(128)} %bitcast.4.slot_ref, bf16[128,4096]{1,0:T(8,128)(2,1)} %broadcast_select_fusion.7.h_ref, f32[2,1,4096]{2,1,0:T(1,128)} %broadcast_in_dim_squeeze.3.gain_ref, bf16[2,4096,1024]{2,1,0:T(8,128)(2,1)} %bitcast.34), custom_call_target="tpu_custom_call" | custom-call | flops 1073741824 | bytes 8388608 | tf_op jit(solution)/shard_map/project/pallas_call | solution.py:48
  61.1 6.4 %collective-permute-start.3 = (bf16[128,1024]{1,0:T(8,128)(2,1)}, bf16[128,1024]{1,0:T(8,128)(2,1)S(1)}, u32[]{:S(2)}, u32[]{:S(2)}) collective-permute-start(bf16[128,1024]{1,0:T(8,128)(2,1)} %get-tuple-element.42.ko_ref.vo_ref), channel_id=1, source_target_pairs={{0,1},{1,2},{2,3},{3,4},{4,5},{5,6},{6,7},{8,9},{9,10},{10,11},{11... | collective-permute-start | bytes 786440 | tf_op jit(solution)/shard_map/ppermute | solution.py:27
  67.5 3.6 collective-permute-done.3.kp_ref.vp_ref
  71.9 6.5 %mix.5 = bf16[128,4096]{1,0:T(8,128)(2,1)} custom-call(bf16[128,4096]{1,0:T(8,128)(2,1)} %broadcast_select_fusion.7.h_ref, bf16[128,4096]{1,0:T(8,128)(2,1)} %get-tuple-element.41.normed_ref, bf16[128,1024]{1,0:T(8,128)(2,1)} %copy-done.20, bf16[128,1024]{1,0:T(8,128)(2,1)} %get-tuple-element.42.ko_ref.vo_ref, bf16[128,1024]{1,0:T(8,128)(2,1)} %copy-done.20, ...), custom_call_target="tpu_custom_call" | custom-call | flops 536870912 | bytes 3145728 | tf_op jit(solution)/shard_map/mix/pallas_call | solution.py:106
  78.4 3.2 collective-permute-start.4
  82.9 16.1 %collective-permute-done.4 = bf16[128,4096]{1,0:T(8,128)(2,1)S(1)} collective-permute-done((bf16[128,4096]{1,0:T(8,128)(2,1)}, bf16[128,4096]{1,0:T(8,128)(2,1)S(1)}, u32[]{:S(2)}, u32[]{:S(2)}) %collective-permute-start.4) | collective-permute-done | bytes 1048608 | tf_op jit(solution)/shard_map/ppermute | solution.py:27
  99.0 4.1 %collective-permute-done.5 = bf16[128,4096]{1,0:T(8,128)(2,1)S(1)} collective-permute-done((bf16[128,4096]{1,0:T(8,128)(2,1)}, bf16[128,4096]{1,0:T(8,128)(2,1)S(1)}, u32[]{:S(2)}, u32[]{:S(2)}) %collective-permute-start.5) | collective-permute-done | bytes 1048608 | tf_op jit(solution)/shard_map/ppermute | solution.py:27
  104.1 6.5 %project.6 = (bf16[128,1024]{1,0:T(8,128)(2,1)}, bf16[128,4096]{1,0:T(8,128)(2,1)}) custom-call(s32[1]{0:T(128)} %bitcast.5.slot_ref, bf16[128,4096]{1,0:T(8,128)(2,1)} %broadcast_select_fusion.11.h_ref, f32[2,1,4096]{2,1,0:T(1,128)} %broadcast_in_dim_squeeze.3.gain_ref, bf16[2,4096,1024]{2,1,0:T(8,128)(2,1)} %bitcast.35), custom_call_target="tpu_custom_call" | custom-call | flops 1073741824 | bytes 8388608 | tf_op jit(solution)/shard_map/project/pallas_call | solution.py:48
  110.6 9.2 %collective-permute-start.6 = (bf16[128,1024]{1,0:T(8,128)(2,1)}, bf16[128,1024]{1,0:T(8,128)(2,1)S(1)}, u32[]{:S(2)}, u32[]{:S(2)}) collective-permute-start(bf16[128,1024]{1,0:T(8,128)(2,1)} %get-tuple-element.44.ko_ref.vo_ref), channel_id=1, source_target_pairs={{0,1},{1,2},{2,3},{3,4},{4,5},{5,6},{6,7},{8,9},{9,10},{10,11},{11... | collective-permute-start | bytes 786440 | tf_op jit(solution)/shard_map/ppermute | solution.py:27
  119.8 3.6 collective-permute-done.6.kp_ref.vp_ref
  124.2 6.5 %mix.6 = bf16[128,4096]{1,0:T(8,128)(2,1)} custom-call(bf16[128,4096]{1,0:T(8,128)(2,1)} %broadcast_select_fusion.11.h_ref, bf16[128,4096]{1,0:T(8,128)(2,1)} %get-tuple-element.43.normed_ref, bf16[128,1024]{1,0:T(8,128)(2,1)} %copy-done.22, bf16[128,1024]{1,0:T(8,128)(2,1)} %get-tuple-element.44.ko_ref.vo_ref, bf16[128,1024]{1,0:T(8,128)(2,1)} %copy-done.22, ...), custom_call_target="tpu_custom_call" | custom-call | flops 536870912 | bytes 3145728 | tf_op jit(solution)/shard_map/mix/pallas_call | solution.py:106
  130.7 4.4 %collective-permute-start.7 = (bf16[128,4096]{1,0:T(8,128)(2,1)}, bf16[128,4096]{1,0:T(8,128)(2,1)}, u32[]{:S(2)}, u32[]{:S(2)}) collective-permute-start(bf16[128,4096]{1,0:T(8,128)(2,1)} %mix.6), channel_id=1, source_target_pairs={{0,8},{8,16},{16,24},{1,9},{9,17},{17,25},{2,10},{10,18},{18,26},{... | collective-permute-start | bytes 3145736 | tf_op jit(solution)/shard_map/ppermute | solution.py:27
  136.4 2.4 broadcast_select_fusion.14.c_ref
  138.8 9.9 %collective-permute-done.7 = bf16[128,4096]{1,0:T(8,128)(2,1)} collective-permute-done((bf16[128,4096]{1,0:T(8,128)(2,1)}, bf16[128,4096]{1,0:T(8,128)(2,1)}, u32[]{:S(2)}, u32[]{:S(2)}) %collective-permute-start.7) | collective-permute-done | bytes 1048608 | tf_op jit(solution)/shard_map/ppermute | solution.py:27
  148.8 5.1 %collective-permute-done.8 = bf16[128,4096]{1,0:T(8,128)(2,1)} collective-permute-done((bf16[128,4096]{1,0:T(8,128)(2,1)}, bf16[128,4096]{1,0:T(8,128)(2,1)}, u32[]{:S(2)}, u32[]{:S(2)}) %collective-permute-start.8) | collective-permute-done | bytes 1048608 | tf_op jit(solution)/shard_map/ppermute | solution.py:27
  153.9 3.7 broadcast_select_fusion
  157.6 6.6 %project.7 = (bf16[128,1024]{1,0:T(8,128)(2,1)}, bf16[128,4096]{1,0:T(8,128)(2,1)}) custom-call(s32[1]{0:T(128)} %bitcast.6.slot_ref, bf16[128,4096]{1,0:T(8,128)(2,1)} %get-tuple-element.88.h_ref, f32[2,1,4096]{2,1,0:T(1,128)} %broadcast_in_dim_squeeze.3.gain_ref, bf16[2,4096,1024]{2,1,0:T(8,128)(2,1)} %bitcast.36), custom_call_target="tpu_custom_call" | custom-call | flops 1073741824 | bytes 8388608 | tf_op jit(solution)/shard_map/project/pallas_call | solution.py:48
  164.3 8.7 %collective-permute-start.9 = (bf16[128,1024]{1,0:T(8,128)(2,1)}, bf16[128,1024]{1,0:T(8,128)(2,1)S(1)}, u32[]{:S(2)}, u32[]{:S(2)}) collective-permute-start(bf16[128,1024]{1,0:T(8,128)(2,1)} %get-tuple-element.46.ko_ref.vo_ref), channel_id=1, source_target_pairs={{0,1},{1,2},{2,3},{3,4},{4,5},{5,6},{6,7},{8,9},{9,10},{10,11},{11... | collective-permute-start | bytes 786440 | tf_op jit(solution)/shard_map/ppermute | solution.py:27
  173.0 2.5 broadcast_select_fusion.1
  175.5 1.9 broadcast_select_fusion.5
  180.3 12.3 %reverse_mix.4 = (bf16[128,4096]{1,0:T(8,128)(2,1)}, bf16[128,512]{1,0:T(8,128)(2,1)}, bf16[128,512]{1,0:T(8,128)(2,1)}, bf16[128,512]{1,0:T(8,128)(2,1)}, bf16[128,512]{1,0:T(8,128)(2,1)}) custom-call(bf16[128,4096]{1,0:T(8,128)(2,1)} %broadcast_select_fusion.14.c_ref, bf16[128,4096]{1,0:T(8,128)(2,1)} %get-tuple-element.107.normed_ref, ...), custom_call_target="tpu_custom_call" | custom-call | flops 1342177280 | bytes 3145728 | tf_op jit(solution)/shard_map/reverse_mix/pallas_call | solution.py:158
  192.6 1.9 collective-permute-start.10
  194.6 1.9 collective-permute-start.11
  196.5 1.8 broadcast_select_fusion.4
  199.1 1.9 collective-permute-done.11.rv_ref
  201.7 9.7 %reverse_project.4 = (bf16[128,4096]{1,0:T(8,128)(2,1)}, bf16[128,1024]{1,0:T(8,128)(2,1)}) custom-call(s32[1]{0:T(128)} %bitcast.6.slot_ref, bf16[128,4096]{1,0:T(8,128)(2,1)} %broadcast_select_fusion.14.c_ref, bf16[128,4096]{1,0:T(8,128)(2,1)} %get-tuple-element.47.dq_ref, bf16[128,4096]{1,0:T(8,128)(2,1)} %get-tuple-element.104.h_ref, ...), custom_call_target="tpu_custom_call" | custom-call | flops 1073741824 | bytes 8388608 | tf_op jit(solution)/shard_map/reverse_project/pallas_call | solution.py:211
  212.7 4.1 %collective-permute-start.13 = (bf16[128,4096]{1,0:T(8,128)(2,1)}, bf16[128,4096]{1,0:T(8,128)(2,1)S(1)}, u32[]{:S(2)}, u32[]{:S(2)}) collective-permute-start(bf16[128,4096]{1,0:T(8,128)(2,1)} %get-tuple-element.52), channel_id=1, source_target_pairs={{0,8},{8,16},{16,24},{1,9},{9,17},{17,25},{2,10},{10,18},{18,26},{... | collective-permute-start | bytes 3145736 | tf_op jit(solution)/shard_map/ppermute | solution.py:27
  216.8 19.1 %collective-permute-done.12 = bf16[128,4096]{1,0:T(8,128)(2,1)S(1)} collective-permute-done((bf16[128,4096]{1,0:T(8,128)(2,1)}, bf16[128,4096]{1,0:T(8,128)(2,1)S(1)}, u32[]{:S(2)}, u32[]{:S(2)}) %collective-permute-start.12) | collective-permute-done | bytes 1048608 | tf_op jit(solution)/shard_map/ppermute | solution.py:27
  235.8 1.9 collective-permute-done.13
  238.8 12.2 %reverse_mix.5 = (bf16[128,4096]{1,0:T(8,128)(2,1)}, bf16[128,512]{1,0:T(8,128)(2,1)}, bf16[128,512]{1,0:T(8,128)(2,1)}, bf16[128,512]{1,0:T(8,128)(2,1)}, bf16[128,512]{1,0:T(8,128)(2,1)}) custom-call(bf16[128,4096]{1,0:T(8,128)(2,1)} %broadcast_select_fusion.10.c_ref, bf16[128,4096]{1,0:T(8,128)(2,1)} %get-tuple-element.106.normed_ref, ...), custom_call_target="tpu_custom_call" | custom-call | flops 1342177280 | bytes 3145728 | tf_op jit(solution)/shard_map/reverse_mix/pallas_call | solution.py:158
  251.0 1.9 collective-permute-start.14
  252.9 1.9 collective-permute-start.15
  254.9 3.6 collective-permute-done.14.rk_ref
  258.5 1.9 collective-permute-done.15.rv_ref
  261.1 9.8 %reverse_project.5 = (bf16[128,4096]{1,0:T(8,128)(2,1)}, bf16[128,1024]{1,0:T(8,128)(2,1)}) custom-call(s32[1]{0:T(128)} %bitcast.5.slot_ref, bf16[128,4096]{1,0:T(8,128)(2,1)} %broadcast_select_fusion.10.c_ref, bf16[128,4096]{1,0:T(8,128)(2,1)} %get-tuple-element.53.dq_ref, bf16[128,4096]{1,0:T(8,128)(2,1)} %get-tuple-element.103.h_ref, ...), custom_call_target="tpu_custom_call" | custom-call | flops 1073741824 | bytes 8388608 | tf_op jit(solution)/shard_map/reverse_project/pallas_call | solution.py:211
  272.1 4.9 %collective-permute-start.17 = (bf16[128,4096]{1,0:T(8,128)(2,1)}, bf16[128,4096]{1,0:T(8,128)(2,1)S(1)}, u32[]{:S(2)}, u32[]{:S(2)}) collective-permute-start(bf16[128,4096]{1,0:T(8,128)(2,1)} %get-tuple-element.58), channel_id=1, source_target_pairs={{0,8},{8,16},{16,24},{1,9},{9,17},{17,25},{2,10},{10,18},{18,26},{... | collective-permute-start | bytes 3145736 | tf_op jit(solution)/shard_map/ppermute | solution.py:27
  277.0 17.3 %collective-permute-done.16 = bf16[128,4096]{1,0:T(8,128)(2,1)S(1)} collective-permute-done((bf16[128,4096]{1,0:T(8,128)(2,1)}, bf16[128,4096]{1,0:T(8,128)(2,1)S(1)}, u32[]{:S(2)}, u32[]{:S(2)}) %collective-permute-start.16) | collective-permute-done | bytes 1048608 | tf_op jit(solution)/shard_map/ppermute | solution.py:27
  294.3 1.9 collective-permute-done.17
  297.3 12.2 %reverse_mix.6 = (bf16[128,4096]{1,0:T(8,128)(2,1)}, bf16[128,512]{1,0:T(8,128)(2,1)}, bf16[128,512]{1,0:T(8,128)(2,1)}, bf16[128,512]{1,0:T(8,128)(2,1)}, bf16[128,512]{1,0:T(8,128)(2,1)}) custom-call(bf16[128,4096]{1,0:T(8,128)(2,1)} %broadcast_select_fusion.6.c_ref, bf16[128,4096]{1,0:T(8,128)(2,1)} %get-tuple-element.105.normed_ref, ...), custom_call_target="tpu_custom_call" | custom-call | flops 1342177280 | bytes 3145728 | tf_op jit(solution)/shard_map/reverse_mix/pallas_call | solution.py:158
  309.4 1.9 collective-permute-start.18
  311.4 1.9 collective-permute-start.19
  313.3 6.5 %mix.7 = bf16[128,4096]{1,0:T(8,128)(2,1)} custom-call(bf16[128,4096]{1,0:T(8,128)(2,1)} %get-tuple-element.88.h_ref, bf16[128,4096]{1,0:T(8,128)(2,1)} %get-tuple-element.45.normed_ref, bf16[128,1024]{1,0:T(8,128)(2,1)} %copy-done.17, bf16[128,1024]{1,0:T(8,128)(2,1)} %get-tuple-element.46.ko_ref.vo_ref, bf16[128,1024]{1,0:T(8,128)(2,1)} %copy-done.17, ...), custom_call_target="tpu_custom_call" | custom-call | flops 536870912 | bytes 3145728 | tf_op jit(solution)/shard_map/mix/pallas_call | solution.py:106
  320.5 9.8 %reverse_project.6 = (bf16[128,4096]{1,0:T(8,128)(2,1)}, bf16[128,1024]{1,0:T(8,128)(2,1)}) custom-call(s32[1]{0:T(128)} %bitcast.4.slot_ref, bf16[128,4096]{1,0:T(8,128)(2,1)} %broadcast_select_fusion.6.c_ref, bf16[128,4096]{1,0:T(8,128)(2,1)} %get-tuple-element.59.dq_ref, bf16[128,4096]{1,0:T(8,128)(2,1)} %get-tuple-element.102.h_ref, ...), custom_call_target="tpu_custom_call" | custom-call | flops 1073741824 | bytes 8388608 | tf_op jit(solution)/shard_map/reverse_project/pallas_call | solution.py:211
  331.6 4.4 %collective-permute-start.21 = (bf16[128,4096]{1,0:T(8,128)(2,1)}, bf16[128,4096]{1,0:T(8,128)(2,1)S(1)}, u32[]{:S(2)}, u32[]{:S(2)}) collective-permute-start(bf16[128,4096]{1,0:T(8,128)(2,1)} %get-tuple-element.64), channel_id=1, source_target_pairs={{0,8},{8,16},{16,24},{1,9},{9,17},{17,25},{2,10},{10,18},{18,26},{... | collective-permute-start | bytes 3145736 | tf_op jit(solution)/shard_map/ppermute | solution.py:27
  336.1 2.8 select_bitcast_fusion.3
  338.9 14.6 %collective-permute-done.20 = bf16[128,4096]{1,0:T(8,128)(2,1)S(1)} collective-permute-done((bf16[128,4096]{1,0:T(8,128)(2,1)}, bf16[128,4096]{1,0:T(8,128)(2,1)S(1)}, u32[]{:S(2)}, u32[]{:S(2)}) %collective-permute-start.20) | collective-permute-done | bytes 1048608 | tf_op jit(solution)/shard_map/ppermute | solution.py:27
  353.4 1.9 collective-permute-done.21
  356.4 12.3 %reverse_mix.7 = (bf16[128,4096]{1,0:T(8,128)(2,1)}, bf16[128,512]{1,0:T(8,128)(2,1)}, bf16[128,512]{1,0:T(8,128)(2,1)}, bf16[128,512]{1,0:T(8,128)(2,1)}, bf16[128,512]{1,0:T(8,128)(2,1)}) custom-call(bf16[128,4096]{1,0:T(8,128)(2,1)} %broadcast_select_fusion.2.c_ref, bf16[128,4096]{1,0:T(8,128)(2,1)} %get-tuple-element.95.normed_ref, ...), custom_call_target="tpu_custom_call" | custom-call | flops 1342177280 | bytes 3145728 | tf_op jit(solution)/shard_map/reverse_mix/pallas_call | solution.py:158
  368.7 1.9 collective-permute-start.22
  370.6 1.9 collective-permute-start.23
  372.6 1.5 maximum_bitcast_fusion
  374.1 5.9 %collective-permute-done.22.rk_ref = bf16[128,512]{1,0:T(8,128)(2,1)S(1)} collective-permute-done((bf16[128,512]{1,0:T(8,128)(2,1)}, bf16[128,512]{1,0:T(8,128)(2,1)S(1)}, u32[]{:S(2)}, u32[]{:S(2)}) %collective-permute-start.22) | collective-permute-done | bytes 131104 | tf_op jit(solution)/shard_map/ppermute | solution.py:27
  380.0 1.9 collective-permute-done.23.rv_ref
  382.6 9.8 %reverse_project.7 = (bf16[128,4096]{1,0:T(8,128)(2,1)}, bf16[128,1024]{1,0:T(8,128)(2,1)}) custom-call(s32[1]{0:T(128)} %bitcast.slot_ref, bf16[128,4096]{1,0:T(8,128)(2,1)} %broadcast_select_fusion.2.c_ref, bf16[128,4096]{1,0:T(8,128)(2,1)} %get-tuple-element.65.dq_ref, bf16[128,4096]{1,0:T(8,128)(2,1)} %get-tuple-element.85.h_ref, ...), custom_call_target="tpu_custom_call" | custom-call | flops 1073741824 | bytes 8388608 | tf_op jit(solution)/shard_map/reverse_project/pallas_call | solution.py:211
  392.4 1.4 select_bitcast_fusion.1
  393.9 1.5 maximum_bitcast_fusion.1
  (109 shorter events, 25.3 us)
Async XLA Ops:
  4.3 11.0 %copy-start.39 = (s32[2,16]{1,0:T(2,128)S(1)}, s32[2,16]{1,0:T(2,128)}, u32[]{:S(2)}) copy-start(s32[2,16]{1,0:T(2,128)} %param.13) | copy-start | bytes 388
  10.8 8.1 %collective-permute-start = (bf16[128,1024]{1,0:T(8,128)(2,1)}, bf16[128,1024]{1,0:T(8,128)(2,1)S(1)}, u32[]{:S(2)}, u32[]{:S(2)}) collective-permute-start(bf16[128,1024]{1,0:T(8,128)(2,1)} %get-tuple-element.40.ko_ref.vo_ref), channel_id=1, source_target_pairs={{0,1},{1,2},{2,3},{3,4},{4,5},{5,6},{6,7},{8,9},{9,10},{10,11},{11... | collective-permute-start | bytes 786440 | tf_op jit(solution)/shard_map/ppermute | solution.py:27
  18.9 0.7 copy-start.18
  26.1 23.4 %collective-permute-start.1 = (bf16[128,4096]{1,0:T(8,128)(2,1)}, bf16[128,4096]{1,0:T(8,128)(2,1)S(1)}, u32[]{:S(2)}, u32[]{:S(2)}) collective-permute-start(bf16[128,4096]{1,0:T(8,128)(2,1)} %mix.4), channel_id=1, source_target_pairs={{0,8},{8,16},{16,24},{1,9},{9,17},{17,25},{2,10},{10,18},{18,26},{... | collective-permute-start | bytes 3145736 | tf_op jit(solution)/shard_map/ppermute | solution.py:27
  29.3 24.2 %collective-permute-start.2 = (bf16[128,4096]{1,0:T(8,128)(2,1)}, bf16[128,4096]{1,0:T(8,128)(2,1)S(1)}, u32[]{:S(2)}, u32[]{:S(2)}) collective-permute-start(bf16[128,4096]{1,0:T(8,128)(2,1)} %mix.4), channel_id=1, source_target_pairs={{8,0},{16,8},{24,16},{9,1},{17,9},{25,17},{10,2},{18,10},{26,18},{... | collective-permute-start | bytes 3145736 | tf_op jit(solution)/shard_map/ppermute | solution.py:27
  61.1 10.0 %collective-permute-start.3 = (bf16[128,1024]{1,0:T(8,128)(2,1)}, bf16[128,1024]{1,0:T(8,128)(2,1)S(1)}, u32[]{:S(2)}, u32[]{:S(2)}) collective-permute-start(bf16[128,1024]{1,0:T(8,128)(2,1)} %get-tuple-element.42.ko_ref.vo_ref), channel_id=1, source_target_pairs={{0,1},{1,2},{2,3},{3,4},{4,5},{5,6},{6,7},{8,9},{9,10},{10,11},{11... | collective-permute-start | bytes 786440 | tf_op jit(solution)/shard_map/ppermute | solution.py:27
  71.1 0.7 copy-start.20
  78.4 20.6 %collective-permute-start.4 = (bf16[128,4096]{1,0:T(8,128)(2,1)}, bf16[128,4096]{1,0:T(8,128)(2,1)S(1)}, u32[]{:S(2)}, u32[]{:S(2)}) collective-permute-start(bf16[128,4096]{1,0:T(8,128)(2,1)} %mix.5), channel_id=1, source_target_pairs={{0,8},{8,16},{16,24},{1,9},{9,17},{17,25},{2,10},{10,18},{18,26},{... | collective-permute-start | bytes 3145736 | tf_op jit(solution)/shard_map/ppermute | solution.py:27
  81.6 21.4 %collective-permute-start.5 = (bf16[128,4096]{1,0:T(8,128)(2,1)}, bf16[128,4096]{1,0:T(8,128)(2,1)S(1)}, u32[]{:S(2)}, u32[]{:S(2)}) collective-permute-start(bf16[128,4096]{1,0:T(8,128)(2,1)} %mix.5), channel_id=1, source_target_pairs={{8,0},{16,8},{24,16},{9,1},{17,9},{25,17},{10,2},{18,10},{26,18},{... | collective-permute-start | bytes 3145736 | tf_op jit(solution)/shard_map/ppermute | solution.py:27
  110.6 12.8 %collective-permute-start.6 = (bf16[128,1024]{1,0:T(8,128)(2,1)}, bf16[128,1024]{1,0:T(8,128)(2,1)S(1)}, u32[]{:S(2)}, u32[]{:S(2)}) collective-permute-start(bf16[128,1024]{1,0:T(8,128)(2,1)} %get-tuple-element.44.ko_ref.vo_ref), channel_id=1, source_target_pairs={{0,1},{1,2},{2,3},{3,4},{4,5},{5,6},{6,7},{8,9},{9,10},{10,11},{11... | collective-permute-start | bytes 786440 | tf_op jit(solution)/shard_map/ppermute | solution.py:27
  123.4 0.7 copy-start.22
  130.7 23.2 %copy-start = (bf16[128,4096]{1,0:T(8,128)(2,1)S(1)}, bf16[128,4096]{1,0:T(8,128)(2,1)}, u32[]{:S(2)}) copy-start(bf16[128,4096]{1,0:T(8,128)(2,1)} %broadcast_select_fusion.3.h_ref) | copy-start | bytes 3145732
  130.7 23.2 %copy-start.1 = (bf16[128,4096]{1,0:T(8,128)(2,1)S(1)}, bf16[128,4096]{1,0:T(8,128)(2,1)}, u32[]{:S(2)}) copy-start(bf16[128,4096]{1,0:T(8,128)(2,1)} %broadcast_select_fusion.7.h_ref) | copy-start | bytes 3145732
  130.7 23.2 %copy-start.2 = (bf16[128,4096]{1,0:T(8,128)(2,1)S(1)}, bf16[128,4096]{1,0:T(8,128)(2,1)}, u32[]{:S(2)}) copy-start(bf16[128,4096]{1,0:T(8,128)(2,1)} %broadcast_select_fusion.11.h_ref) | copy-start | bytes 3145732
  130.7 18.1 %collective-permute-start.7 = (bf16[128,4096]{1,0:T(8,128)(2,1)}, bf16[128,4096]{1,0:T(8,128)(2,1)}, u32[]{:S(2)}, u32[]{:S(2)}) collective-permute-start(bf16[128,4096]{1,0:T(8,128)(2,1)} %mix.6), channel_id=1, source_target_pairs={{0,8},{8,16},{16,24},{1,9},{9,17},{17,25},{2,10},{10,18},{18,26},{... | collective-permute-start | bytes 3145736 | tf_op jit(solution)/shard_map/ppermute | solution.py:27
  135.1 18.8 %collective-permute-start.8 = (bf16[128,4096]{1,0:T(8,128)(2,1)}, bf16[128,4096]{1,0:T(8,128)(2,1)}, u32[]{:S(2)}, u32[]{:S(2)}) collective-permute-start(bf16[128,4096]{1,0:T(8,128)(2,1)} %mix.6), channel_id=1, source_target_pairs={{8,0},{16,8},{24,16},{9,1},{17,9},{25,17},{10,2},{18,10},{26,18},{... | collective-permute-start | bytes 3145736 | tf_op jit(solution)/shard_map/ppermute | solution.py:27
  157.6 15.4 %copy-start.8 = (bf16[128,4096]{1,0:T(8,128)(2,1)S(1)}, bf16[128,4096]{1,0:T(8,128)(2,1)}, u32[]{:S(2)}) copy-start(bf16[128,4096]{1,0:T(8,128)(2,1)} %get-tuple-element.39.normed_ref) | copy-start | bytes 3145732
  157.6 15.4 %copy-start.9 = (bf16[128,4096]{1,0:T(8,128)(2,1)S(1)}, bf16[128,4096]{1,0:T(8,128)(2,1)}, u32[]{:S(2)}) copy-start(bf16[128,4096]{1,0:T(8,128)(2,1)} %get-tuple-element.41.normed_ref) | copy-start | bytes 3145732
  157.6 15.4 %copy-start.10 = (bf16[128,4096]{1,0:T(8,128)(2,1)S(1)}, bf16[128,4096]{1,0:T(8,128)(2,1)}, u32[]{:S(2)}) copy-start(bf16[128,4096]{1,0:T(8,128)(2,1)} %get-tuple-element.43.normed_ref) | copy-start | bytes 3145732
  164.3 14.0 %collective-permute-start.9 = (bf16[128,1024]{1,0:T(8,128)(2,1)}, bf16[128,1024]{1,0:T(8,128)(2,1)S(1)}, u32[]{:S(2)}, u32[]{:S(2)}) collective-permute-start(bf16[128,1024]{1,0:T(8,128)(2,1)} %get-tuple-element.46.ko_ref.vo_ref), channel_id=1, source_target_pairs={{0,1},{1,2},{2,3},{3,4},{4,5},{5,6},{6,7},{8,9},{9,10},{10,11},{11... | collective-permute-start | bytes 786440 | tf_op jit(solution)/shard_map/ppermute | solution.py:27
  175.5 2.0 copy-start.13
  175.5 2.0 copy-start.14
  175.5 2.0 copy-start.15
  175.5 2.0 copy-start.16
  175.5 2.8 copy-start.19
  175.5 2.8 copy-start.21
  175.5 2.7 copy-start.23
  178.3 2.1 copy-start.17
  180.3 16.2 %copy-start.3 = (bf16[128,4096]{1,0:T(8,128)(2,1)S(1)}, bf16[128,4096]{1,0:T(8,128)(2,1)}, u32[]{:S(2)}) copy-start(bf16[128,4096]{1,0:T(8,128)(2,1)} %get-tuple-element.86) | copy-start | bytes 3145732
  180.3 16.2 %copy-start.4 = (bf16[128,4096]{1,0:T(8,128)(2,1)S(1)}, bf16[128,4096]{1,0:T(8,128)(2,1)}, u32[]{:S(2)}) copy-start(bf16[128,4096]{1,0:T(8,128)(2,1)} %get-tuple-element.87) | copy-start | bytes 3145732
  192.6 6.5 %collective-permute-start.10 = (bf16[128,512]{1,0:T(8,128)(2,1)}, bf16[128,512]{1,0:T(8,128)(2,1)S(1)}, u32[]{:S(2)}, u32[]{:S(2)}) collective-permute-start(bf16[128,512]{1,0:T(8,128)(2,1)} %get-tuple-element.49), channel_id=1, source_target_pairs={{1,0},{2,1},{3,2},{4,3},{5,4},{6,5},{7,6},{9,8},{10,9},{11,10},{12... | collective-permute-start | bytes 393224 | tf_op jit(solution)/shard_map/ppermute | solution.py:27
  194.6 6.5 %collective-permute-start.11 = (bf16[128,512]{1,0:T(8,128)(2,1)}, bf16[128,512]{1,0:T(8,128)(2,1)S(1)}, u32[]{:S(2)}, u32[]{:S(2)}) collective-permute-start(bf16[128,512]{1,0:T(8,128)(2,1)} %get-tuple-element.51), channel_id=1, source_target_pairs={{1,0},{2,1},{3,2},{4,3},{5,4},{6,5},{7,6},{9,8},{10,9},{11,10},{12... | collective-permute-start | bytes 393224 | tf_op jit(solution)/shard_map/ppermute | solution.py:27
  199.1 1.9 copy-start.33
  201.1 0.7 copy-start.36
  211.4 24.4 %collective-permute-start.12 = (bf16[128,4096]{1,0:T(8,128)(2,1)}, bf16[128,4096]{1,0:T(8,128)(2,1)S(1)}, u32[]{:S(2)}, u32[]{:S(2)}) collective-permute-start(bf16[128,4096]{1,0:T(8,128)(2,1)} %get-tuple-element.52), channel_id=1, source_target_pairs={{8,0},{16,8},{24,16},{9,1},{17,9},{25,17},{10,2},{18,10},{26,18},{... | collective-permute-start | bytes 3145736 | tf_op jit(solution)/shard_map/ppermute | solution.py:27
  212.7 25.0 %collective-permute-start.13 = (bf16[128,4096]{1,0:T(8,128)(2,1)}, bf16[128,4096]{1,0:T(8,128)(2,1)S(1)}, u32[]{:S(2)}, u32[]{:S(2)}) collective-permute-start(bf16[128,4096]{1,0:T(8,128)(2,1)} %get-tuple-element.52), channel_id=1, source_target_pairs={{0,8},{8,16},{16,24},{1,9},{9,17},{17,25},{2,10},{10,18},{18,26},{... | collective-permute-start | bytes 3145736 | tf_op jit(solution)/shard_map/ppermute | solution.py:27
  251.0 7.5 %collective-permute-start.14 = (bf16[128,512]{1,0:T(8,128)(2,1)}, bf16[128,512]{1,0:T(8,128)(2,1)S(1)}, u32[]{:S(2)}, u32[]{:S(2)}) collective-permute-start(bf16[128,512]{1,0:T(8,128)(2,1)} %get-tuple-element.55), channel_id=1, source_target_pairs={{1,0},{2,1},{3,2},{4,3},{5,4},{6,5},{7,6},{9,8},{10,9},{11,10},{12... | collective-permute-start | bytes 393224 | tf_op jit(solution)/shard_map/ppermute | solution.py:27
  252.9 7.5 %collective-permute-start.15 = (bf16[128,512]{1,0:T(8,128)(2,1)}, bf16[128,512]{1,0:T(8,128)(2,1)S(1)}, u32[]{:S(2)}, u32[]{:S(2)}) collective-permute-start(bf16[128,512]{1,0:T(8,128)(2,1)} %get-tuple-element.57), channel_id=1, source_target_pairs={{1,0},{2,1},{3,2},{4,3},{5,4},{6,5},{7,6},{9,8},{10,9},{11,10},{12... | collective-permute-start | bytes 393224 | tf_op jit(solution)/shard_map/ppermute | solution.py:27
  258.5 1.9 copy-start.37
  260.4 0.7 copy-start.38
  270.8 23.5 %collective-permute-start.16 = (bf16[128,4096]{1,0:T(8,128)(2,1)}, bf16[128,4096]{1,0:T(8,128)(2,1)S(1)}, u32[]{:S(2)}, u32[]{:S(2)}) collective-permute-start(bf16[128,4096]{1,0:T(8,128)(2,1)} %get-tuple-element.58), channel_id=1, source_target_pairs={{8,0},{16,8},{24,16},{9,1},{17,9},{25,17},{10,2},{18,10},{26,18},{... | collective-permute-start | bytes 3145736 | tf_op jit(solution)/shard_map/ppermute | solution.py:27
  272.1 24.1 %collective-permute-start.17 = (bf16[128,4096]{1,0:T(8,128)(2,1)}, bf16[128,4096]{1,0:T(8,128)(2,1)S(1)}, u32[]{:S(2)}, u32[]{:S(2)}) collective-permute-start(bf16[128,4096]{1,0:T(8,128)(2,1)} %get-tuple-element.58), channel_id=1, source_target_pairs={{0,8},{8,16},{16,24},{1,9},{9,17},{17,25},{2,10},{10,18},{18,26},{... | collective-permute-start | bytes 3145736 | tf_op jit(solution)/shard_map/ppermute | solution.py:27
  309.4 10.4 %collective-permute-start.18 = (bf16[128,512]{1,0:T(8,128)(2,1)}, bf16[128,512]{1,0:T(8,128)(2,1)S(1)}, u32[]{:S(2)}, u32[]{:S(2)}) collective-permute-start(bf16[128,512]{1,0:T(8,128)(2,1)} %get-tuple-element.61), channel_id=1, source_target_pairs={{1,0},{2,1},{3,2},{4,3},{5,4},{6,5},{7,6},{9,8},{10,9},{11,10},{12... | collective-permute-start | bytes 393224 | tf_op jit(solution)/shard_map/ppermute | solution.py:27
  311.4 8.5 %collective-permute-start.19 = (bf16[128,512]{1,0:T(8,128)(2,1)}, bf16[128,512]{1,0:T(8,128)(2,1)S(1)}, u32[]{:S(2)}, u32[]{:S(2)}) collective-permute-start(bf16[128,512]{1,0:T(8,128)(2,1)} %get-tuple-element.63), channel_id=1, source_target_pairs={{1,0},{2,1},{3,2},{4,3},{5,4},{6,5},{7,6},{9,8},{10,9},{11,10},{12... | collective-permute-start | bytes 393224 | tf_op jit(solution)/shard_map/ppermute | solution.py:27
  319.8 0.7 copy-start.31
  319.8 0.7 copy-start.34
  320.5 15.5 %copy-start.5 = (bf16[128,4096]{1,0:T(8,128)(2,1)S(1)}, bf16[128,4096]{1,0:T(8,128)(2,1)}, u32[]{:S(2)}) copy-start(bf16[128,4096]{1,0:T(8,128)(2,1)} %mix.4) | copy-start | bytes 3145732
  320.5 15.5 %copy-start.6 = (bf16[128,4096]{1,0:T(8,128)(2,1)S(1)}, bf16[128,4096]{1,0:T(8,128)(2,1)}, u32[]{:S(2)}) copy-start(bf16[128,4096]{1,0:T(8,128)(2,1)} %mix.5) | copy-start | bytes 3145732
  320.5 15.5 %copy-start.7 = (bf16[128,4096]{1,0:T(8,128)(2,1)S(1)}, bf16[128,4096]{1,0:T(8,128)(2,1)}, u32[]{:S(2)}) copy-start(bf16[128,4096]{1,0:T(8,128)(2,1)} %mix.6) | copy-start | bytes 3145732
  330.3 23.1 %collective-permute-start.20 = (bf16[128,4096]{1,0:T(8,128)(2,1)}, bf16[128,4096]{1,0:T(8,128)(2,1)S(1)}, u32[]{:S(2)}, u32[]{:S(2)}) collective-permute-start(bf16[128,4096]{1,0:T(8,128)(2,1)} %get-tuple-element.64), channel_id=1, source_target_pairs={{8,0},{16,8},{24,16},{9,1},{17,9},{25,17},{10,2},{18,10},{26,18},{... | collective-permute-start | bytes 3145736 | tf_op jit(solution)/shard_map/ppermute | solution.py:27
  331.6 23.7 %collective-permute-start.21 = (bf16[128,4096]{1,0:T(8,128)(2,1)}, bf16[128,4096]{1,0:T(8,128)(2,1)S(1)}, u32[]{:S(2)}, u32[]{:S(2)}) collective-permute-start(bf16[128,4096]{1,0:T(8,128)(2,1)} %get-tuple-element.64), channel_id=1, source_target_pairs={{0,8},{8,16},{16,24},{1,9},{9,17},{17,25},{2,10},{10,18},{18,26},{... | collective-permute-start | bytes 3145736 | tf_op jit(solution)/shard_map/ppermute | solution.py:27
  356.4 16.1 %copy-start.11 = (bf16[1,128,4096]{2,1,0:T(8,128)(2,1)S(1)}, bf16[1,128,4096]{2,1,0:T(8,128)(2,1)}, u32[]{:S(2)}) copy-start(bf16[1,128,4096]{2,1,0:T(8,128)(2,1)} %get-tuple-element.100) | copy-start | bytes 3145732
  356.4 16.1 %copy-start.12 = (bf16[1,128,4096]{2,1,0:T(8,128)(2,1)S(1)}, bf16[1,128,4096]{2,1,0:T(8,128)(2,1)}, u32[]{:S(2)}) copy-start(bf16[1,128,4096]{2,1,0:T(8,128)(2,1)} %get-tuple-element.101) | copy-start | bytes 3145732
  368.7 11.3 %collective-permute-start.22 = (bf16[128,512]{1,0:T(8,128)(2,1)}, bf16[128,512]{1,0:T(8,128)(2,1)S(1)}, u32[]{:S(2)}, u32[]{:S(2)}) collective-permute-start(bf16[128,512]{1,0:T(8,128)(2,1)} %get-tuple-element.67), channel_id=1, source_target_pairs={{1,0},{2,1},{3,2},{4,3},{5,4},{6,5},{7,6},{9,8},{10,9},{11,10},{12... | collective-permute-start | bytes 393224 | tf_op jit(solution)/shard_map/ppermute | solution.py:27
  370.6 11.3 %collective-permute-start.23 = (bf16[128,512]{1,0:T(8,128)(2,1)}, bf16[128,512]{1,0:T(8,128)(2,1)S(1)}, u32[]{:S(2)}, u32[]{:S(2)}) collective-permute-start(bf16[128,512]{1,0:T(8,128)(2,1)} %get-tuple-element.69), channel_id=1, source_target_pairs={{1,0},{2,1},{3,2},{4,3},{5,4},{6,5},{7,6},{9,8},{10,9},{11,10},{12... | collective-permute-start | bytes 393224 | tf_op jit(solution)/shard_map/ppermute | solution.py:27
  380.0 1.9 copy-start.32
  381.9 0.7 copy-start.35
  382.6 9.8 %copy-start.24 = (bf16[128,4096]{1,0:T(8,128)(2,1)S(1)}, bf16[128,4096]{1,0:T(8,128)(2,1)}, u32[]{:S(2)}) copy-start(bf16[128,4096]{1,0:T(8,128)(2,1)} %get-tuple-element.52) | copy-start | bytes 3145732
  382.6 9.8 %copy-start.25 = (bf16[128,4096]{1,0:T(8,128)(2,1)S(1)}, bf16[128,4096]{1,0:T(8,128)(2,1)}, u32[]{:S(2)}) copy-start(bf16[128,4096]{1,0:T(8,128)(2,1)} %get-tuple-element.58) | copy-start | bytes 3145732
  382.6 9.9 %copy-start.26 = (bf16[128,4096]{1,0:T(8,128)(2,1)S(1)}, bf16[128,4096]{1,0:T(8,128)(2,1)}, u32[]{:S(2)}) copy-start(bf16[128,4096]{1,0:T(8,128)(2,1)} %get-tuple-element.64) | copy-start | bytes 3145732
  393.9 1.5 copy-start.27
  393.9 1.5 copy-start.28
  393.9 1.5 copy-start.29
  393.9 1.5 copy-start.30
where the time goes:
time: 403 us; the launch traced here: 396 us
  Pallas kernels  140 us (35%)
  waiting for transfers between devices  140 us (35%)
  starting transfers between devices  76.1 us (19%)
  other arithmetic  32.5 us (8%)
  local copies, waits for them, and re-layouts  6.26 us (2%)
    ppermute x24, waiting for transfers between devices, passed_along(): return lax.ppermute(block, axis, route)  140 us
    ppermute x24, starting transfers between devices, passed_along(): return lax.ppermute(block, axis, route)  76.1 us
    pallas_call x4, Pallas kernels, reverse_mix(): pl.pallas_call(reverse_kernel, grid=(KV_HEADS,), in_specs=[block, block]...  49 us
    pallas_call x4, Pallas kernels, reverse_project(): pl.pallas_call(functools.partial(reverse_project_kernel, steps), grid_spe...  39.1 us
    pallas_call x4, Pallas kernels, mix(): pl.pallas_call(mix_kernel, grid=(KV_HEADS,), in_specs=[block, block] + he...  26.1 us
    pallas_call x4, Pallas kernels, project(): pl.pallas_call(project_kernel, grid_spec=pltpu.PrefetchScalarGridSpec(num...  26 us
    select_n x7, other arithmetic, per_device(): jnp.where(down, a, b)  12.8 us
  transfers between devices with their start and end apart: 24, of which 21 were waited for; matrix products, arithmetic and copies ran while one was open for 4% of the time, Pallas kernels for 2%

commit v1 on v0

v1 whole, which is shorter than its diff:
```python
import functools
import math

import jax
import jax.numpy as jnp
from jax import lax
from jax.experimental import pallas as pl
from jax.experimental.pallas import tpu as pltpu
from jax.sharding import PartitionSpec as P

HEADS = 32
HEAD_DIM = 128
KV_HEADS = 4
GROUP = HEADS // KV_HEADS
SCALE = 1.0 / math.sqrt(HEAD_DIM)
LOG2E = math.log2(math.e)

epsilon = 1e-05

F32 = jnp.float32
BF16 = jnp.bfloat16
MESH = pl.DeviceIdType.MESH


def dot(a, b, dims):
    return lax.dot_general(a, b, (dims, ((), ())), preferred_element_type=F32)


def relay_kernel(
    count, shards,
    lengths_ref, xa_ref, xb_ref, ga_ref, gb_ref, gains_ref, weights_ref,
    acts_ref, ingrad_ref, kvgrad_ref,
    wbuf, hbuf, nbuf, kv, wsave, cbuf, outc, dqbuf, gnbuf, gbuf, bias, rstd_buf,
    dsend, drecv, downs, dtot,
    x_sem, w_sem, c_sem, g_sem, gs_sem, gr_sem,
    zs_sem, zr_sem, ss_sem, sr_sem, cs_sem, cr_sem, ds_sem, dr_sem,
    act_sem, ing_sem, kvg_sem,
):
    section = lax.axis_index("section")
    shard = lax.axis_index("seq")
    rows = xa_ref.shape[0]
    width = xa_ref.shape[1]
    tile = width // KV_HEADS
    half = KV_HEADS * HEAD_DIM
    near = lax.div(2 * section, count)
    near_depth = section + near * (count - 1 - 2 * section)
    far = 1 - near
    far_depth = count - 1 - near_depth
    following = lax.rem(shard + 1, shards)
    preceding = lax.rem(shard + shards - 1, shards)

    def depth_of(d):
        return section + d * (count - 1 - 2 * section)

    def x_copy(d, t):
        ref = (xa_ref, xb_ref)[d]
        return pltpu.make_async_copy(
            ref.at[:, pl.ds(t * tile, tile)], hbuf.at[d, 0, t], x_sem.at[d, t]
        )

    def grad_copy(d, t):
        ref = (ga_ref, gb_ref)[d]
        return pltpu.make_async_copy(
            ref.at[:, pl.ds(t * tile, tile)], cbuf.at[d, t], c_sem.at[d, t]
        )

    def weight_copy(d, k, part):
        return pltpu.make_async_copy(
            weights_ref.at[0, d, :, pl.ds(pl.multiple_of(part * half + k * HEAD_DIM, HEAD_DIM), HEAD_DIM)],
            wbuf.at[d, k, :, pl.ds(part * HEAD_DIM, HEAD_DIM)],
            w_sem.at[d, k, part],
        )

    def gain_copy(distance):
        return pltpu.make_async_remote_copy(
            src_ref=gains_ref,
            dst_ref=gbuf.at[section],
            send_sem=gs_sem.at[distance - 1],
            recv_sem=gr_sem.at[distance - 1],
            device_id={"section": lax.rem(section + distance, count)},
            device_id_type=MESH,
        )

    def z_copy(d, l, k):
        own = kv.at[d, l, k, :, pl.ds(rows, rows), :]
        return pltpu.make_async_remote_copy(
            src_ref=own, dst_ref=own, send_sem=zs_sem.at[d, l, k], recv_sem=zr_sem.at[d, l, k],
            device_id={"section": section + 1 - 2 * d}, device_id_type=MESH,
        )

    def s_copy(d, l, k):
        return pltpu.make_async_remote_copy(
            src_ref=kv.at[d, l, k, :, pl.ds(rows, rows), :],
            dst_ref=kv.at[d, l, k, :, pl.ds(0, rows), :],
            send_sem=ss_sem.at[d, l, k], recv_sem=sr_sem.at[d, l, k],
            device_id={"seq": following}, device_id_type=MESH,
        )

    def c_copy(d, t):
        return pltpu.make_async_remote_copy(
            src_ref=outc.at[d, t], dst_ref=cbuf.at[d, t],
            send_sem=cs_sem.at[d, t], recv_sem=cr_sem.at[d, t],
            device_id={"section": section - 1 + 2 * d}, device_id_type=MESH,
        )

    def d_copy(d, k):
        return pltpu.make_async_remote_copy(
            src_ref=dsend.at[d, k], dst_ref=drecv.at[d, k],
            send_sem=ds_sem.at[d, k], recv_sem=dr_sem.at[d, k],
            device_id={"seq": preceding}, device_id_type=MESH,
        )

    def column_slice(t):
        return pl.ds(pl.multiple_of(t * tile, tile), tile)

    def act_copy(d, parity, t):
        return pltpu.make_async_copy(
            hbuf.at[d, parity, t], acts_ref.at[d, 0, :, column_slice(t)], act_sem.at[d, t]
        )

    def ing_copy(d, t):
        return pltpu.make_async_copy(
            outc.at[d, t], ingrad_ref.at[d, 0, :, column_slice(t)], ing_sem.at[d, t]
        )

    def kvg_copy(d, k, part):
        start = pl.multiple_of(part * half + k * HEAD_DIM, HEAD_DIM)
        return pltpu.make_async_copy(
            dtot.at[d, k, :, pl.ds(part * HEAD_DIM, HEAD_DIM)],
            kvgrad_ref.at[d, 0, :, pl.ds(start, HEAD_DIM)],
            kvg_sem.at[d, k, part],
        )

    for t in range(KV_HEADS):
        x_copy(0, t).start()
        x_copy(1, t).start()
    own_gain = pltpu.make_async_copy(gains_ref, gbuf.at[section], g_sem)
    own_gain.start()
    for d in (near, far):
        for k in range(KV_HEADS):
            for part in range(2):
                weight_copy(d, k, part).start()
    for d, last in ((0, count - 1), (1, 0)):
        @pl.when(section == last)
        def _():
            for t in range(KV_HEADS):
                grad_copy(d, t).start()

    barrier = pltpu.get_barrier_semaphore()
    for neighbour in (following, preceding):
        pl.semaphore_signal(barrier, inc=1, device_id={"seq": neighbour}, device_id_type=MESH)
    for distance in range(1, count):
        pl.semaphore_signal(
            barrier, inc=1, device_id={"section": lax.rem(section + distance, count)},
            device_id_type=MESH,
        )

    key_places = (shard - 1) * rows + lax.broadcasted_iota(jnp.int32, (2 * rows, rows), 0)
    places = shard * rows + lax.broadcasted_iota(jnp.int32, (2 * rows, rows), 1)
    for d in range(2):
        end = jnp.int32(0)
        docs_k = jnp.zeros((2 * rows, rows), jnp.int32)
        docs_q = jnp.zeros((2 * rows, rows), jnp.int32)
        for j in range(lengths_ref.shape[1]):
            end = end + lengths_ref[d, j]
            docs_k = docs_k + jnp.where(key_places >= end, 1, 0)
            docs_q = docs_q + jnp.where(places >= end, 1, 0)
        allowed = (docs_k == docs_q) & (key_places <= places) & (key_places >= 0)
        bias[d] = jnp.where(allowed, 0.0, -1e30).astype(F32)

    pl.semaphore_wait(barrier, count + 1)
    for distance in range(1, count):
        gain_copy(distance).start()
    for t in range(KV_HEADS):
        x_copy(0, t).wait()
        x_copy(1, t).wait()
    own_gain.wait()

    def normalize(d, l, parity):
        home = l + d * (count - 1 - 2 * l)
        squares = jnp.zeros((rows, HEAD_DIM), F32)
        for t in range(KV_HEADS):
            for g in range(GROUP):
                part = hbuf[d, parity, t, :, g * HEAD_DIM:(g + 1) * HEAD_DIM].astype(F32)
                squares = squares + part * part
        rstd = lax.rsqrt(jnp.sum(squares, axis=-1, keepdims=True) * (1.0 / width) + epsilon)
        rstd = jnp.broadcast_to(rstd, (rows, HEAD_DIM))
        rstd_buf[d] = rstd
        for t in range(KV_HEADS):
            for g in range(GROUP):
                cols = slice(g * HEAD_DIM, (g + 1) * HEAD_DIM)
                gain = gbuf[home, d, :, t * tile + g * HEAD_DIM:t * tile + (g + 1) * HEAD_DIM]
                part = hbuf[d, parity, t, :, cols].astype(F32)
                nbuf[d, t, :, cols] = (part * rstd * gain).astype(BF16)

    def project(d, depth):
        normalize(d, depth, lax.rem(depth, 2))

        def chunk(k, carry):
            weight_copy(d, k, 0).wait()
            weight_copy(d, k, 1).wait()
            pair = jnp.zeros((rows, 2 * HEAD_DIM), F32)
            for t in range(KV_HEADS):
                pair = pair + dot(
                    nbuf[d, t], wbuf[d, k, t * tile:(t + 1) * tile, :], ((1,), (0,))
                )
            pair = pair.astype(BF16)
            kv[d, depth, k, 0, rows:, :] = pair[:, :HEAD_DIM]
            kv[d, depth, k, 1, rows:, :] = pair[:, HEAD_DIM:]

            @pl.when(depth < count - 1)
            def _():
                z_copy(d, depth, k).start()

            s_copy(d, depth, k).start()
            return carry

        lax.fori_loop(0, KV_HEADS, chunk, 0)

    def mix(d, l, depth):
        parity = lax.rem(l, 2)

        @pl.when(l < depth)
        def _():
            normalize(d, l, parity)

        def arrive(k):
            @pl.when(l < depth)
            def _():
                z_copy(d, l, k).wait_recv()

                @pl.when(depth < count - 1)
                def _():
                    z_copy(d, l, k).start()

                s_copy(d, l, k).start()

        arrive(0)

        def chunk(k, carry):
            @pl.when(k + 1 < KV_HEADS)
            def _():
                arrive(k + 1)

            s_copy(d, l, k).wait_recv()
            keys = kv[d, l, k, 0]
            values = kv[d, l, k, 1]
            masked = bias[d]
            for g in range(GROUP):
                cols = slice(g * HEAD_DIM, (g + 1) * HEAD_DIM)
                scores = dot(keys, nbuf[d, k, :, cols], ((1,), (1,))) + masked
                powers = jnp.exp2((scores - jnp.max(scores, axis=0, keepdims=True)) * (SCALE * LOG2E))
                weights = (powers * (1.0 / jnp.sum(powers, axis=0, keepdims=True))).astype(BF16)
                wsave[d, k, g] = weights
                mixture = dot(weights, values, ((0,), (0,)))
                hbuf[d, 1 - parity, k, :, cols] = (
                    hbuf[d, parity, k, :, cols].astype(F32) + mixture
                ).astype(BF16)

            @pl.when(l == depth)
            def _():
                act_copy(d, 1 - parity, k).start()

            return carry

        lax.fori_loop(0, KV_HEADS, chunk, 0)

    def forward(v, carry):
        p = near_depth
        is_near = (v < p) | (v == 2 * p)
        d = jnp.where(is_near, near, far)
        depth = jnp.where(is_near, near_depth, far_depth)
        l = jnp.where(v < p, v, jnp.where(v < 2 * p, v - p, jnp.where(v == 2 * p, p, v - p - 1)))

        @pl.when((v == p) | (v == count))
        def _():
            pd = jnp.where(v == p, near, far)
            project(pd, jnp.where(v == p, near_depth, far_depth))

        @pl.when(v == 0)
        def _():
            for distance in range(1, count):
                gain_copy(distance).wait_recv()

        mix(d, l, depth)
        return carry

    lax.fori_loop(0, count + 1, forward, 0)

    def backward(i, carry):
        d = jnp.where(i == 0, far, near)
        depth = jnp.where(i == 0, far_depth, near_depth)
        parity = lax.rem(depth, 2)

        def chunk(k, inner_carry):
            @pl.when(depth < count - 1)
            def _():
                c_copy(d, k).wait_recv()

            @pl.when(depth == count - 1)
            def _():
                pltpu.make_async_copy(cbuf.at[d, k], cbuf.at[d, k], c_sem.at[d, k]).wait()

            keys = kv[d, depth, k, 0]
            values = kv[d, depth, k, 1]
            grads, queries, probs, cots = [], [], [], []
            for g in range(GROUP):
                cols = slice(g * HEAD_DIM, (g + 1) * HEAD_DIM)
                query = nbuf[d, k, :, cols]
                cot = cbuf[d, k, :, cols]
                weights = wsave[d, k, g]
                wide = weights.astype(F32)
                grad_w = dot(values, cot, ((1,), (1,)))
                mean = jnp.sum(grad_w * wide, axis=0, keepdims=True)
                grad_s = (wide * (grad_w - mean) * SCALE).astype(BF16)
                dqbuf[k, :, cols] = dot(grad_s, keys, ((0,), (0,))).astype(BF16)
                grads.append(grad_s)
                queries.append(query)
                probs.append(weights)
                cots.append(cot)
            grad_k = dot(
                jnp.concatenate(grads, axis=1), jnp.concatenate(queries, axis=0), ((1,), (0,))
            )
            grad_v = dot(
                jnp.concatenate(probs, axis=1), jnp.concatenate(cots, axis=0), ((1,), (0,))
            )
            dsend[d, k, 0] = grad_k[:rows].astype(BF16)
            dsend[d, k, 1] = grad_v[:rows].astype(BF16)
            downs[k, 0] = grad_k[rows:].astype(BF16)
            downs[k, 1] = grad_v[rows:].astype(BF16)
            d_copy(d, k).start()
            return inner_carry

        lax.fori_loop(0, KV_HEADS, chunk, 0)

        for k in range(KV_HEADS):
            d_copy(d, k).wait_recv()
            for part in range(2):
                total = downs[k, part].astype(F32) + drecv[d, k, part].astype(F32)
                dtot[d, k, :, part * HEAD_DIM:(part + 1) * HEAD_DIM] = total.astype(BF16)
                kvg_copy(d, k, part).start()

        home = section
        rstd = rstd_buf[d]

        def grad_tile(t, inner):
            grad = jnp.zeros((rows, tile), F32)
            start = pl.multiple_of(t * tile, tile)
            for k in range(KV_HEADS):
                grad = grad + dot(
                    dtot[d, k], wbuf[d, k, pl.ds(start, tile), :], ((1,), (1,))
                )
            for g in range(GROUP):
                cols = slice(g * HEAD_DIM, (g + 1) * HEAD_DIM)
                gain = gbuf[home, d, :, pl.ds(pl.multiple_of(start + g * HEAD_DIM, HEAD_DIM), HEAD_DIM)]
                grad_n = (grad[:, cols] + dqbuf[t, :, cols].astype(F32)) * gain
                gnbuf[t, :, cols] = grad_n
                inner = inner + grad_n * hbuf[d, parity, t, :, cols].astype(F32)
            return inner

        inner = lax.fori_loop(0, KV_HEADS, grad_tile, jnp.zeros((rows, HEAD_DIM), F32))
        inner = jnp.broadcast_to(jnp.sum(inner, axis=-1, keepdims=True), (rows, HEAD_DIM))
        factor = inner * (1.0 / width) * rstd * rstd * rstd

        def total_tile(t, inner_carry):
            for g in range(GROUP):
                cols = slice(g * HEAD_DIM, (g + 1) * HEAD_DIM)
                grad_h = gnbuf[t, :, cols] * rstd - hbuf[d, parity, t, :, cols].astype(F32) * factor
                outc[d, t, :, cols] = (cbuf[d, t, :, cols].astype(F32) + grad_h).astype(BF16)

            @pl.when(depth > 0)
            def _():
                c_copy(d, t).start()

            ing_copy(d, t).start()
            return inner_carry

        lax.fori_loop(0, KV_HEADS, total_tile, 0)
        return carry

    lax.fori_loop(0, 2, backward, 0)

    for distance in range(1, count):
        gain_copy(distance).wait_send()
    for d in range(2):
        depth = depth_of(d)

        def layer_drain(l, carry):
            for k in range(KV_HEADS):
                @pl.when(depth < count - 1)
                def _():
                    z_copy(d, l, k).wait_send()

                s_copy(d, l, k).wait_send()
            return carry

        lax.fori_loop(0, depth + 1, layer_drain, 0)
        for k in range(KV_HEADS):
            d_copy(d, k).wait_send()

            @pl.when(depth > 0)
            def _():
                c_copy(d, k).wait_send()

            act_copy(d, lax.rem(depth + 1, 2), k).wait()
            ing_copy(d, k).wait()
            kvg_copy(d, k, 0).wait()
            kvg_copy(d, k, 1).wait()


def per_device(x_a, x_b, grad_a, grad_b, gains, kv_weights, doc_lengths):
    count = lax.axis_size("section")
    shards = lax.axis_size("seq")
    rows, width = x_a.shape
    pair_width = kv_weights.shape[-1]
    tile = width // KV_HEADS
    gains = gains[0][:, None, :]
    dma = pltpu.SemaphoreType.DMA
    anywhere = pl.BlockSpec(memory_space=pl.ANY)
    return pl.pallas_call(
        functools.partial(relay_kernel, count, shards),
        in_specs=[pl.BlockSpec(memory_space=pltpu.SMEM)] + [anywhere] * 6,
        out_specs=[anywhere] * 3,
        out_shape=[
            jax.ShapeDtypeStruct((2, 1, rows, width), BF16),
            jax.ShapeDtypeStruct((2, 1, rows, width), BF16),
            jax.ShapeDtypeStruct((2, 1, rows, pair_width), BF16),
        ],
        scratch_shapes=[
            pltpu.VMEM((2, KV_HEADS, width, 2 * HEAD_DIM), BF16),
            pltpu.VMEM((2, 2, KV_HEADS, rows, tile), BF16),
            pltpu.VMEM((2, KV_HEADS, rows, tile), BF16),
            pltpu.VMEM((2, count, KV_HEADS, 2, 2 * rows, HEAD_DIM), BF16),
            pltpu.VMEM((2, KV_HEADS, GROUP, 2 * rows, rows), BF16),
            pltpu.VMEM((2, KV_HEADS, rows, tile), BF16),
            pltpu.VMEM((2, KV_HEADS, rows, tile), BF16),
            pltpu.VMEM((KV_HEADS, rows, tile), BF16),
            pltpu.VMEM((KV_HEADS, rows, tile), F32),
            pltpu.VMEM((count, 2, 1, width), F32),
            pltpu.VMEM((2, 2 * rows, rows), F32),
            pltpu.VMEM((2, rows, HEAD_DIM), F32),
            pltpu.VMEM((2, KV_HEADS, 2, rows, HEAD_DIM), BF16),
            pltpu.VMEM((2, KV_HEADS, 2, rows, HEAD_DIM), BF16),
            pltpu.VMEM((KV_HEADS, 2, rows, HEAD_DIM), BF16),
            pltpu.VMEM((2, KV_HEADS, rows, 2 * HEAD_DIM), BF16),
            dma((2, KV_HEADS)),
            dma((2, KV_HEADS, 2)),
            dma((2, KV_HEADS)),
            dma(()),
            dma((count - 1,)),
            dma((count - 1,)),
            dma((2, count, KV_HEADS)),
            dma((2, count, KV_HEADS)),
            dma((2, count, KV_HEADS)),
            dma((2, count, KV_HEADS)),
            dma((2, KV_HEADS)),
            dma((2, KV_HEADS)),
            dma((2, KV_HEADS)),
            dma((2, KV_HEADS)),
            dma((2, KV_HEADS)),
            dma((2, KV_HEADS)),
            dma((2, KV_HEADS, 2)),
        ],
        compiler_params=pltpu.CompilerParams(
            collective_id=0, has_side_effects=True, vmem_limit_bytes=60 * 1024 * 1024
        ),
        name="relay",
    )(doc_lengths, x_a, x_b, grad_a, grad_b, gains, kv_weights)


def solution(mesh):
    in_specs = (
        P("seq", None),
        P("seq", None),
        P("seq", None),
        P("seq", None),
        P("section", None, None),
        P("section", None, None, None),
        P(),
    )
    out_specs = (
        P(None, "section", "seq", None),
        P(None, "section", "seq", None),
        P(None, "section", "seq", None),
    )
    return jax.shard_map(
        per_device, mesh=mesh, in_specs=in_specs, out_specs=out_specs, check_vma=False
    )
```

time: 403 us -> 175 us (0.43); the launches traced: 396 us -> 174 us
  waiting for transfers between devices: 140 us -> 0 us
  starting transfers between devices: 76.1 us -> 0 us
  other arithmetic: 32.5 us -> 0 us
  Pallas kernels: 140 us -> 167 us
    ppermute x24 -> x0, waiting for transfers between devices: 140 us -> none  [passed_along(): return lax.ppermute(block, axis, route)]
    ppermute x24 -> x0, starting transfers between devices: 76.1 us -> none  [passed_along(): return lax.ppermute(block, axis, route)]
    pallas_call x16 -> x1, Pallas kernels: 140 us -> 167 us  [per_device(): pl.pallas_call(functools.partial(relay_kernel, count, shards), in_specs=[...]
    select_n x15 -> x0, other arithmetic: 24 us -> none  [the longest x7 12.8 us: per_device(): jnp.where(down, a, b)]
    another operation x4 -> x0, other arithmetic: 4.49 us -> none  [the longest x1 2.78 us: per_device(): acts_out = jnp.stack([saved['down'][4], saved['up'][4]])[:, None]]
  transfers between devices with their start and end apart: 24 -> 0, of which waited for: 21 -> 0; matrix products, arithmetic and copies ran while one was open for 4% -> 0% of each run, Pallas kernels for 2% -> 0%
where the time goes in v1:
time: 175 us; the launch traced here: 174 us
  Pallas kernels  167 us (95%)
  local copies, waits for them, and re-layouts  6.87 us (4%)
    pallas_call x1, Pallas kernels, per_device(): pl.pallas_call(functools.partial(relay_kernel, count, shards), in_specs=[...  167 us
    unnamed x7, local copies, waits for them, and re-layouts  5.47 us

profile of v1, /device:TPU:1, one launch (start us, length us, event | category | flops | bytes accessed | tf_op | source)
XLA Modules:
  0.0 174.5 jit_solution(7460401393313375693)
XLA Ops:
  0.6 1.4 broadcast_in_dim_squeeze.3.gains_ref
  2.0 167.0 %relay.1 = (bf16[2,1,128,4096]{3,2,1,0:T(8,128)(2,1)}, bf16[2,1,128,4096]{3,2,1,0:T(8,128)(2,1)}, bf16[2,1,128,1024]{3,2,1,0:T(8,128)(2,1)}) custom-call(s32[2,16]{1,0:T(2,128)} %lengths_ref.1, bf16[128,4096]{1,0:T(8,128)(2,1)} %xa_ref.1, bf16[128,4096]{1,0:T(8,128)(2,1)} %xb_ref.1, bf16[128,4096]{1,0:T(8,128)(2,1)} %ga_ref.1, bf16[128,4096]{1,0:T(8,128)(2,1)} %gb_ref.1, ...), custom_call_target="tpu_custom_call" | custom-call | tf_op jit(solution)/shard_map/relay/pallas_call | solution.py:420
  169.0 0.0 copy-start
  169.0 3.3 %copy.13 = bf16[2,1,128,4096]{3,2,1,0:T(8,128)(2,1)} copy(bf16[2,1,128,4096]{3,2,1,0:T(8,128)(2,1)} %get-tuple-element.6) | data formatting | bytes 4194304
  172.3 0.0 copy-done
  172.3 0.0 copy-start.1
  172.3 1.3 copy.14
  173.6 0.1 copy-done.1
  173.7 0.8 copy.15
Async XLA Ops:
  169.0 3.3 %copy-start = (bf16[2,1,128,4096]{3,2,1,0:T(8,128)(2,1)S(1)}, bf16[2,1,128,4096]{3,2,1,0:T(8,128)(2,1)}, u32[]{:S(2)}) copy-start(bf16[2,1,128,4096]{3,2,1,0:T(8,128)(2,1)} %get-tuple-element.7) | copy-start | bytes 6291460
  172.3 1.4 copy-start.1

commit v2 on v1

--- a/solution.py
+++ b/solution.py
@@ -31,7 +31,7 @@
     lengths_ref, xa_ref, xb_ref, ga_ref, gb_ref, gains_ref, weights_ref,
     acts_ref, ingrad_ref, kvgrad_ref,
     wbuf, hbuf, nbuf, kv, wsave, cbuf, outc, dqbuf, gnbuf, gbuf, bias, rstd_buf,
-    dsend, drecv, downs, dtot,
+    dsend, drecv, downs, dtot, triangle, squares_buf,
     x_sem, w_sem, c_sem, g_sem, gs_sem, gr_sem,
     zs_sem, zr_sem, ss_sem, sr_sem, cs_sem, cr_sem, ds_sem, dr_sem,
     act_sem, ing_sem, kvg_sem,
@@ -73,7 +73,7 @@
 
     def gain_copy(distance):
         return pltpu.make_async_remote_copy(
-            src_ref=gains_ref,
+            src_ref=gains_ref.at[0],
             dst_ref=gbuf.at[section],
             send_sem=gs_sem.at[distance - 1],
             recv_sem=gr_sem.at[distance - 1],
@@ -134,7 +134,7 @@
     for t in range(KV_HEADS):
         x_copy(0, t).start()
         x_copy(1, t).start()
-    own_gain = pltpu.make_async_copy(gains_ref, gbuf.at[section], g_sem)
+    own_gain = pltpu.make_async_copy(gains_ref.at[0], gbuf.at[section], g_sem)
     own_gain.start()
     for d in (near, far):
         for k in range(KV_HEADS):
@@ -167,6 +167,12 @@
             docs_q = docs_q + jnp.where(places >= end, 1, 0)
         allowed = (docs_k == docs_q) & (key_places <= places) & (key_places >= 0)
         bias[d] = jnp.where(allowed, 0.0, -1e30).astype(F32)
+    sublane = lax.broadcasted_iota(jnp.int32, (rows, rows), 0)
+    lane = lax.broadcasted_iota(jnp.int32, (rows, rows), 1)
+    triangle[0] = jnp.where(sublane > lane, 1.0, 0.0).astype(BF16)
+    triangle[1] = jnp.where(sublane <= lane, 1.0, 0.0).astype(BF16)
+    triangle[2] = jnp.where(lane > sublane, 1.0, 0.0).astype(BF16)
+    triangle[3] = jnp.where(lane <= sublane, 1.0, 0.0).astype(BF16)
 
     pl.semaphore_wait(barrier, count + 1)
     for distance in range(1, count):
@@ -176,20 +182,28 @@
         x_copy(1, t).wait()
     own_gain.wait()
 
+    def gain_of(home, d, cols):
+        return jnp.where(d == 0, gbuf[home, 0:1, cols], gbuf[home, 1:2, cols])
+
     def normalize(d, l, parity):
         home = l + d * (count - 1 - 2 * l)
-        squares = jnp.zeros((rows, HEAD_DIM), F32)
-        for t in range(KV_HEADS):
-            for g in range(GROUP):
-                part = hbuf[d, parity, t, :, g * HEAD_DIM:(g + 1) * HEAD_DIM].astype(F32)
-                squares = squares + part * part
-        rstd = lax.rsqrt(jnp.sum(squares, axis=-1, keepdims=True) * (1.0 / width) + epsilon)
-        rstd = jnp.broadcast_to(rstd, (rows, HEAD_DIM))
+
+        @pl.when(l == 0)
+        def _():
+            squares = jnp.zeros((rows, HEAD_DIM), F32)
+            for t in range(KV_HEADS):
+                for g in range(GROUP):
+                    part = hbuf[d, parity, t, :, g * HEAD_DIM:(g + 1) * HEAD_DIM].astype(F32)
+                    squares = squares + part * part
+            squares_buf[d] = squares
+
+        square_mean = jnp.sum(squares_buf[d], axis=-1, keepdims=True) * (1.0 / width)
+        rstd = jnp.broadcast_to(lax.rsqrt(square_mean + epsilon), (rows, HEAD_DIM))
         rstd_buf[d] = rstd
         for t in range(KV_HEADS):
             for g in range(GROUP):
                 cols = slice(g * HEAD_DIM, (g + 1) * HEAD_DIM)
-                gain = gbuf[home, d, :, t * tile + g * HEAD_DIM:t * tile + (g + 1) * HEAD_DIM]
+                gain = gain_of(home, d, slice(t * tile + g * HEAD_DIM, t * tile + (g + 1) * HEAD_DIM))
                 part = hbuf[d, parity, t, :, cols].astype(F32)
                 nbuf[d, t, :, cols] = (part * rstd * gain).astype(BF16)
 
@@ -199,12 +213,8 @@
         def chunk(k, carry):
             weight_copy(d, k, 0).wait()
             weight_copy(d, k, 1).wait()
-            pair = jnp.zeros((rows, 2 * HEAD_DIM), F32)
-            for t in range(KV_HEADS):
-                pair = pair + dot(
-                    nbuf[d, t], wbuf[d, k, t * tile:(t + 1) * tile, :], ((1,), (0,))
-                )
-            pair = pair.astype(BF16)
+            normed = jnp.concatenate([nbuf[d, t] for t in range(KV_HEADS)], axis=1)
+            pair = dot(normed, wbuf[d, k], ((1,), (0,))).astype(BF16)
             kv[d, depth, k, 0, rows:, :] = pair[:, :HEAD_DIM]
             kv[d, depth, k, 1, rows:, :] = pair[:, HEAD_DIM:]
 
@@ -224,6 +234,8 @@
         def _():
             normalize(d, l, parity)
 
+        squares_buf[d] = jnp.zeros((rows, HEAD_DIM), F32)
+
         def arrive(k):
             @pl.when(l < depth)
             def _():
@@ -245,17 +257,20 @@
             s_copy(d, l, k).wait_recv()
             keys = kv[d, l, k, 0]
             values = kv[d, l, k, 1]
-            masked = bias[d]
+            spreads = []
             for g in range(GROUP):
-                cols = slice(g * HEAD_DIM, (g + 1) * HEAD_DIM)
-                scores = dot(keys, nbuf[d, k, :, cols], ((1,), (1,))) + masked
+                both = dot(keys, nbuf[d, k, :, g * HEAD_DIM:(g + 1) * HEAD_DIM], ((1,), (1,)))
+                scores = jnp.maximum(both[:rows] + bias[d, :rows, :], both[rows:] + bias[d, rows:, :])
                 powers = jnp.exp2((scores - jnp.max(scores, axis=0, keepdims=True)) * (SCALE * LOG2E))
                 weights = (powers * (1.0 / jnp.sum(powers, axis=0, keepdims=True))).astype(BF16)
                 wsave[d, k, g] = weights
-                mixture = dot(weights, values, ((0,), (0,)))
-                hbuf[d, 1 - parity, k, :, cols] = (
-                    hbuf[d, parity, k, :, cols].astype(F32) + mixture
-                ).astype(BF16)
+                turned = weights.T
+                spreads.append(jnp.concatenate([turned * triangle[2], turned * triangle[3]], axis=1))
+            for g in range(GROUP):
+                cols = slice(g * HEAD_DIM, (g + 1) * HEAD_DIM)
+                total = hbuf[d, parity, k, :, cols].astype(F32) + dot(spreads[g], values, ((1,), (0,)))
+                hbuf[d, 1 - parity, k, :, cols] = total.astype(BF16)
+                squares_buf[d] += total * total
 
             @pl.when(l == depth)
             def _():
@@ -303,27 +318,38 @@
 
             keys = kv[d, depth, k, 0]
             values = kv[d, depth, k, 1]
-            grads, queries, probs, cots = [], [], [], []
+            earlier_s, own_s, earlier_w, own_w, queries, cots, spreads = [], [], [], [], [], [], []
+            own_first = lax.broadcasted_iota(jnp.int32, (rows, rows), 0) <= (
+                lax.broadcasted_iota(jnp.int32, (rows, rows), 1)
+            )
             for g in range(GROUP):
                 cols = slice(g * HEAD_DIM, (g + 1) * HEAD_DIM)
-                query = nbuf[d, k, :, cols]
                 cot = cbuf[d, k, :, cols]
+                both = dot(values, cot, ((1,), (1,)))
                 weights = wsave[d, k, g]
                 wide = weights.astype(F32)
-                grad_w = dot(values, cot, ((1,), (1,)))
-                mean = jnp.sum(grad_w * wide, axis=0, keepdims=True)
-                grad_s = (wide * (grad_w - mean) * SCALE).astype(BF16)
-                dqbuf[k, :, cols] = dot(grad_s, keys, ((0,), (0,))).astype(BF16)
-                grads.append(grad_s)
-                queries.append(query)
-                probs.append(weights)
+                grad_w = jnp.where(own_first, both[rows:], both[:rows]) * wide
+                mean = jnp.sum(grad_w, axis=0, keepdims=True)
+                grad_s = ((grad_w - wide * mean) * SCALE).astype(BF16)
+                earlier_s.append(grad_s * triangle[0])
+                own_s.append(grad_s * triangle[1])
+                earlier_w.append(weights * triangle[0])
+                own_w.append(weights * triangle[1])
+                queries.append(nbuf[d, k, :, cols])
                 cots.append(cot)
-            grad_k = dot(
-                jnp.concatenate(grads, axis=1), jnp.concatenate(queries, axis=0), ((1,), (0,))
+                turned = grad_s.T
+                spreads.append(jnp.concatenate([turned * triangle[2], turned * triangle[3]], axis=1))
+            for g in range(GROUP):
+                cols = slice(g * HEAD_DIM, (g + 1) * HEAD_DIM)
+                dqbuf[k, :, cols] = dot(spreads[g], keys, ((1,), (0,))).astype(BF16)
+            all_s = jnp.concatenate(
+                [jnp.concatenate(earlier_s, axis=1), jnp.concatenate(own_s, axis=1)], axis=0
             )
-            grad_v = dot(
-                jnp.concatenate(probs, axis=1), jnp.concatenate(cots, axis=0), ((1,), (0,))
+            all_w = jnp.concatenate(
+                [jnp.concatenate(earlier_w, axis=1), jnp.concatenate(own_w, axis=1)], axis=0
             )
+            grad_k = dot(all_s, jnp.concatenate(queries, axis=0), ((1,), (0,)))
+            grad_v = dot(all_w, jnp.concatenate(cots, axis=0), ((1,), (0,)))
             dsend[d, k, 0] = grad_k[:rows].astype(BF16)
             dsend[d, k, 1] = grad_v[:rows].astype(BF16)
             downs[k, 0] = grad_k[rows:].astype(BF16)
@@ -344,18 +370,19 @@
         rstd = rstd_buf[d]
 
         def grad_tile(t, inner):
-            grad = jnp.zeros((rows, tile), F32)
-            start = pl.multiple_of(t * tile, tile)
-            for k in range(KV_HEADS):
-                grad = grad + dot(
-                    dtot[d, k], wbuf[d, k, pl.ds(start, tile), :], ((1,), (1,))
+            pairs = jnp.concatenate([dtot[d, k] for k in range(KV_HEADS)], axis=1)
+            step = 2 * HEAD_DIM
+            for u in range(tile // step):
+                start = pl.multiple_of(t * tile + u * step, step)
+                weights = jnp.concatenate(
+                    [wbuf[d, k, pl.ds(start, step), :] for k in range(KV_HEADS)], axis=1
                 )
-            for g in range(GROUP):
-                cols = slice(g * HEAD_DIM, (g + 1) * HEAD_DIM)
-                gain = gbuf[home, d, :, pl.ds(pl.multiple_of(start + g * HEAD_DIM, HEAD_DIM), HEAD_DIM)]
-                grad_n = (grad[:, cols] + dqbuf[t, :, cols].astype(F32)) * gain
+                cols = slice(u * step, (u + 1) * step)
+                gain = gain_of(home, d, pl.ds(start, step))
+                grad_n = (dot(pairs, weights, ((1,), (1,))) + dqbuf[t, :, cols].astype(F32)) * gain
                 gnbuf[t, :, cols] = grad_n
-                inner = inner + grad_n * hbuf[d, parity, t, :, cols].astype(F32)
+                product = grad_n * hbuf[d, parity, t, :, cols].astype(F32)
+                inner = inner + product[:, :HEAD_DIM] + product[:, HEAD_DIM:]
             return inner
 
         inner = lax.fori_loop(0, KV_HEADS, grad_tile, jnp.zeros((rows, HEAD_DIM), F32))
@@ -414,7 +441,6 @@
     rows, width = x_a.shape
     pair_width = kv_weights.shape[-1]
     tile = width // KV_HEADS
-    gains = gains[0][:, None, :]
     dma = pltpu.SemaphoreType.DMA
     anywhere = pl.BlockSpec(memory_space=pl.ANY)
     return pl.pallas_call(
@@ -431,18 +457,20 @@
             pltpu.VMEM((2, 2, KV_HEADS, rows, tile), BF16),
             pltpu.VMEM((2, KV_HEADS, rows, tile), BF16),
             pltpu.VMEM((2, count, KV_HEADS, 2, 2 * rows, HEAD_DIM), BF16),
-            pltpu.VMEM((2, KV_HEADS, GROUP, 2 * rows, rows), BF16),
+            pltpu.VMEM((2, KV_HEADS, GROUP, rows, rows), BF16),
             pltpu.VMEM((2, KV_HEADS, rows, tile), BF16),
             pltpu.VMEM((2, KV_HEADS, rows, tile), BF16),
             pltpu.VMEM((KV_HEADS, rows, tile), BF16),
             pltpu.VMEM((KV_HEADS, rows, tile), F32),
-            pltpu.VMEM((count, 2, 1, width), F32),
+            pltpu.VMEM((count, 2, width), F32),
             pltpu.VMEM((2, 2 * rows, rows), F32),
             pltpu.VMEM((2, rows, HEAD_DIM), F32),
             pltpu.VMEM((2, KV_HEADS, 2, rows, HEAD_DIM), BF16),
             pltpu.VMEM((2, KV_HEADS, 2, rows, HEAD_DIM), BF16),
             pltpu.VMEM((KV_HEADS, 2, rows, HEAD_DIM), BF16),
             pltpu.VMEM((2, KV_HEADS, rows, 2 * HEAD_DIM), BF16),
+            pltpu.VMEM((4, rows, rows), BF16),
+            pltpu.VMEM((2, rows, HEAD_DIM), F32),
             dma((2, KV_HEADS)),
             dma((2, KV_HEADS, 2)),
             dma((2, KV_HEADS)),

time: 175 us -> 165 us (0.943)
  Pallas kernels: 167 us -> 158 us
    pallas_call x1, Pallas kernels: 167 us -> 158 us  [per_device(): pl.pallas_call(functools.partial(relay_kernel, count, shards), in_specs=[...]
where the time goes in v2:
time: 165 us; the launch traced here: 164 us
  Pallas kernels  158 us (96%)
  local copies, waits for them, and re-layouts  5.47 us (3%)
    pallas_call x1, Pallas kernels, per_device(): pl.pallas_call(functools.partial(relay_kernel, count, shards), in_specs=[...  158 us
    unnamed x7, local copies, waits for them, and re-layouts  5.47 us

profile of v2, /device:TPU:1, one launch (start us, length us, event | category | flops | bytes accessed | tf_op | source)
XLA Modules:
  0.0 164.4 jit_solution(16706058993537683748)
XLA Ops:
  0.6 158.3 %relay.1 = (bf16[2,1,128,4096]{3,2,1,0:T(8,128)(2,1)}, bf16[2,1,128,4096]{3,2,1,0:T(8,128)(2,1)}, bf16[2,1,128,1024]{3,2,1,0:T(8,128)(2,1)}) custom-call(s32[2,16]{1,0:T(2,128)} %lengths_ref.1, bf16[128,4096]{1,0:T(8,128)(2,1)} %xa_ref.1, bf16[128,4096]{1,0:T(8,128)(2,1)} %xb_ref.1, bf16[128,4096]{1,0:T(8,128)(2,1)} %ga_ref.1, bf16[128,4096]{1,0:T(8,128)(2,1)} %gb_ref.1, ...), custom_call_target="tpu_custom_call" | custom-call | tf_op jit(solution)/shard_map/relay/pallas_call | solution.py:446
  158.9 0.0 copy-start
  158.9 3.3 %copy.13 = bf16[2,1,128,4096]{3,2,1,0:T(8,128)(2,1)} copy(bf16[2,1,128,4096]{3,2,1,0:T(8,128)(2,1)} %get-tuple-element.6) | data formatting | bytes 4194304
  162.2 0.0 copy-done
  162.2 0.0 copy-start.1
  162.2 1.3 copy.14
  163.5 0.1 copy-done.1
  163.6 0.8 copy.15
Async XLA Ops:
  158.9 3.3 %copy-start = (bf16[2,1,128,4096]{3,2,1,0:T(8,128)(2,1)S(1)}, bf16[2,1,128,4096]{3,2,1,0:T(8,128)(2,1)}, u32[]{:S(2)}) copy-start(bf16[2,1,128,4096]{3,2,1,0:T(8,128)(2,1)} %get-tuple-element.7) | copy-start | bytes 6291460
  162.2 1.4 copy-start.1

commit v3 on v2

--- a/solution.py
+++ b/solution.py
@@ -14,6 +14,7 @@
 GROUP = HEADS // KV_HEADS
 SCALE = 1.0 / math.sqrt(HEAD_DIM)
 LOG2E = math.log2(math.e)
+PIECES = 8
 
 epsilon = 1e-05
 
@@ -30,11 +31,12 @@
     count, shards,
     lengths_ref, xa_ref, xb_ref, ga_ref, gb_ref, gains_ref, weights_ref,
     acts_ref, ingrad_ref, kvgrad_ref,
-    wbuf, hbuf, nbuf, kv, wsave, cbuf, outc, dqbuf, gnbuf, gbuf, bias, rstd_buf,
+    wbuf, hbuf, nbuf, kv, wsave, cbuf, dqbuf, gnbuf, gbuf, bias, rstd_buf,
     dsend, drecv, downs, dtot, triangle, squares_buf,
     x_sem, w_sem, c_sem, g_sem, gs_sem, gr_sem,
     zs_sem, zr_sem, ss_sem, sr_sem, cs_sem, cr_sem, ds_sem, dr_sem,
     act_sem, ing_sem, kvg_sem,
+    bs_sem, ps_sem, pr_sem, ys_sem, yr_sem, es_sem, er_sem,
 ):
     section = lax.axis_index("section")
     shard = lax.axis_index("seq")
@@ -48,6 +50,12 @@
     far_depth = count - 1 - near_depth
     following = lax.rem(shard + 1, shards)
     preceding = lax.rem(shard + shards - 1, shards)
+    core = lax.rem(shard, 2)
+    side = lax.div(2 * shard, shards)
+    sibling = shard + 1 - 2 * core
+    opposite = lax.rem(shard + shards // 2, shards)
+    extra = 2
+    piece = width // PIECES
 
     def depth_of(d):
         return section + d * (count - 1 - 2 * section)
@@ -96,18 +104,49 @@
             device_id={"seq": following}, device_id_type=MESH,
         )
 
-    def c_copy(d, t):
-        return pltpu.make_async_remote_copy(
-            src_ref=outc.at[d, t], dst_ref=cbuf.at[d, t],
+    def c_copy(d, t, slot):
+        return pltpu.make_async_remote_copy(
+            src_ref=cbuf.at[slot, t], dst_ref=cbuf.at[d, t],
             send_sem=cs_sem.at[d, t], recv_sem=cr_sem.at[d, t],
             device_id={"section": section - 1 + 2 * d}, device_id_type=MESH,
         )
 
-    def d_copy(d, k):
-        return pltpu.make_async_remote_copy(
-            src_ref=dsend.at[d, k], dst_ref=drecv.at[d, k],
-            send_sem=ds_sem.at[d, k], recv_sem=dr_sem.at[d, k],
+    def d_copy(slot, k):
+        return pltpu.make_async_remote_copy(
+            src_ref=dsend.at[slot, k], dst_ref=drecv.at[slot, k],
+            send_sem=ds_sem.at[slot, k], recv_sem=dr_sem.at[slot, k],
             device_id={"seq": preceding}, device_id_type=MESH,
+        )
+
+    def back_copy(k):
+        own = kv.at[near, 1, k, :, pl.ds(rows, rows), :]
+        return pltpu.make_async_remote_copy(
+            src_ref=own, dst_ref=own, send_sem=bs_sem.at[k], recv_sem=zr_sem.at[near, 1, k],
+            device_id={"section": section - 1 + 2 * near}, device_id_type=MESH,
+        )
+
+    def piece_of(slot, on_side, on_core, i):
+        return wbuf.at[slot, 2 * on_side + on_core, pl.ds(pl.multiple_of(i * piece, piece), piece), :]
+
+    def quarter_copy(i):
+        return pltpu.make_async_remote_copy(
+            src_ref=piece_of(near, side, core, i), dst_ref=piece_of(extra, side, core, i),
+            send_sem=ps_sem.at[i], recv_sem=pr_sem.at[i],
+            device_id={"section": section - 1 + 2 * near}, device_id_type=MESH,
+        )
+
+    def opposite_copy(i, on_side):
+        ref = piece_of(extra, on_side, core, i)
+        return pltpu.make_async_remote_copy(
+            src_ref=ref, dst_ref=ref, send_sem=ys_sem.at[i], recv_sem=yr_sem.at[i],
+            device_id={"seq": opposite}, device_id_type=MESH,
+        )
+
+    def sibling_copy(i, part, on_core):
+        ref = piece_of(extra, side + part * (1 - 2 * side), on_core, i)
+        return pltpu.make_async_remote_copy(
+            src_ref=ref, dst_ref=ref, send_sem=es_sem.at[part, i], recv_sem=er_sem.at[part, i],
+            device_id={"seq": sibling}, device_id_type=MESH,
         )
 
     def column_slice(t):
@@ -120,7 +159,7 @@
 
     def ing_copy(d, t):
         return pltpu.make_async_copy(
-            outc.at[d, t], ingrad_ref.at[d, 0, :, column_slice(t)], ing_sem.at[d, t]
+            cbuf.at[3 + d, t], ingrad_ref.at[d, 0, :, column_slice(t)], ing_sem.at[d, t]
         )
 
     def kvg_copy(d, k, part):
@@ -147,7 +186,7 @@
                 grad_copy(d, t).start()
 
     barrier = pltpu.get_barrier_semaphore()
-    for neighbour in (following, preceding):
+    for neighbour in (following, preceding, opposite):
         pl.semaphore_signal(barrier, inc=1, device_id={"seq": neighbour}, device_id_type=MESH)
     for distance in range(1, count):
         pl.semaphore_signal(
@@ -155,28 +194,6 @@
             device_id_type=MESH,
         )
 
-    key_places = (shard - 1) * rows + lax.broadcasted_iota(jnp.int32, (2 * rows, rows), 0)
-    places = shard * rows + lax.broadcasted_iota(jnp.int32, (2 * rows, rows), 1)
-    for d in range(2):
-        end = jnp.int32(0)
-        docs_k = jnp.zeros((2 * rows, rows), jnp.int32)
-        docs_q = jnp.zeros((2 * rows, rows), jnp.int32)
-        for j in range(lengths_ref.shape[1]):
-            end = end + lengths_ref[d, j]
-            docs_k = docs_k + jnp.where(key_places >= end, 1, 0)
-            docs_q = docs_q + jnp.where(places >= end, 1, 0)
-        allowed = (docs_k == docs_q) & (key_places <= places) & (key_places >= 0)
-        bias[d] = jnp.where(allowed, 0.0, -1e30).astype(F32)
-    sublane = lax.broadcasted_iota(jnp.int32, (rows, rows), 0)
-    lane = lax.broadcasted_iota(jnp.int32, (rows, rows), 1)
-    triangle[0] = jnp.where(sublane > lane, 1.0, 0.0).astype(BF16)
-    triangle[1] = jnp.where(sublane <= lane, 1.0, 0.0).astype(BF16)
-    triangle[2] = jnp.where(lane > sublane, 1.0, 0.0).astype(BF16)
-    triangle[3] = jnp.where(lane <= sublane, 1.0, 0.0).astype(BF16)
-
-    pl.semaphore_wait(barrier, count + 1)
-    for distance in range(1, count):
-        gain_copy(distance).start()
     for t in range(KV_HEADS):
         x_copy(0, t).wait()
         x_copy(1, t).wait()
@@ -185,7 +202,7 @@
     def gain_of(home, d, cols):
         return jnp.where(d == 0, gbuf[home, 0:1, cols], gbuf[home, 1:2, cols])
 
-    def normalize(d, l, parity):
+    def normalize(d, l, parity, slot):
         home = l + d * (count - 1 - 2 * l)
 
         @pl.when(l == 0)
@@ -199,16 +216,38 @@
 
         square_mean = jnp.sum(squares_buf[d], axis=-1, keepdims=True) * (1.0 / width)
         rstd = jnp.broadcast_to(lax.rsqrt(square_mean + epsilon), (rows, HEAD_DIM))
-        rstd_buf[d] = rstd
+        rstd_buf[slot] = rstd
         for t in range(KV_HEADS):
             for g in range(GROUP):
                 cols = slice(g * HEAD_DIM, (g + 1) * HEAD_DIM)
                 gain = gain_of(home, d, slice(t * tile + g * HEAD_DIM, t * tile + (g + 1) * HEAD_DIM))
                 part = hbuf[d, parity, t, :, cols].astype(F32)
-                nbuf[d, t, :, cols] = (part * rstd * gain).astype(BF16)
+                nbuf[slot, t, :, cols] = (part * rstd * gain).astype(BF16)
+
+    def make_masks():
+        key_places = (shard - 1) * rows + lax.broadcasted_iota(jnp.int32, (2 * rows, rows), 0)
+        places = shard * rows + lax.broadcasted_iota(jnp.int32, (2 * rows, rows), 1)
+        for d in range(2):
+            end = jnp.int32(0)
+            docs_k = jnp.zeros((2 * rows, rows), jnp.int32)
+            docs_q = jnp.zeros((2 * rows, rows), jnp.int32)
+            for j in range(lengths_ref.shape[1]):
+                end = end + lengths_ref[d, j]
+                docs_k = docs_k + jnp.where(key_places >= end, 1, 0)
+                docs_q = docs_q + jnp.where(places >= end, 1, 0)
+            allowed = (docs_k == docs_q) & (key_places <= places) & (key_places >= 0)
+            bias[d] = jnp.where(allowed, 0.0, -1e30).astype(F32)
+        sublane = lax.broadcasted_iota(jnp.int32, (rows, rows), 0)
+        lane = lax.broadcasted_iota(jnp.int32, (rows, rows), 1)
+        triangle[0] = jnp.where(sublane > lane, 1.0, 0.0).astype(BF16)
+        triangle[1] = jnp.where(sublane <= lane, 1.0, 0.0).astype(BF16)
+        triangle[2] = jnp.where(lane > sublane, 1.0, 0.0).astype(BF16)
+        triangle[3] = jnp.where(lane <= sublane, 1.0, 0.0).astype(BF16)
 
     def project(d, depth):
-        normalize(d, depth, lax.rem(depth, 2))
+        @pl.when(depth > 0)
+        def _():
+            normalize(d, depth, lax.rem(depth, 2), d)
 
         def chunk(k, carry):
             weight_copy(d, k, 0).wait()
@@ -223,16 +262,29 @@
                 z_copy(d, depth, k).start()
 
             s_copy(d, depth, k).start()
+
+            @pl.when(depth == 1)
+            def _():
+                back_copy(k).start()
+
             return carry
 
         lax.fori_loop(0, KV_HEADS, chunk, 0)
+
+    def softmax(d, l, k, slot, g):
+        both = dot(kv[d, l, k, 0], nbuf[slot, k, :, g * HEAD_DIM:(g + 1) * HEAD_DIM], ((1,), (1,)))
+        scores = jnp.maximum(both[:rows] + bias[d, :rows, :], both[rows:] + bias[d, rows:, :])
+        powers = jnp.exp2((scores - jnp.max(scores, axis=0, keepdims=True)) * (SCALE * LOG2E))
+        weights = (powers * (1.0 / jnp.sum(powers, axis=0, keepdims=True))).astype(BF16)
+        wsave[slot, k, g] = weights
+        return weights
 
     def mix(d, l, depth):
         parity = lax.rem(l, 2)
 
         @pl.when(l < depth)
         def _():
-            normalize(d, l, parity)
+            normalize(d, l, parity, d)
 
         squares_buf[d] = jnp.zeros((rows, HEAD_DIM), F32)
 
@@ -255,15 +307,10 @@
                 arrive(k + 1)
 
             s_copy(d, l, k).wait_recv()
-            keys = kv[d, l, k, 0]
             values = kv[d, l, k, 1]
             spreads = []
             for g in range(GROUP):
-                both = dot(keys, nbuf[d, k, :, g * HEAD_DIM:(g + 1) * HEAD_DIM], ((1,), (1,)))
-                scores = jnp.maximum(both[:rows] + bias[d, :rows, :], both[rows:] + bias[d, rows:, :])
-                powers = jnp.exp2((scores - jnp.max(scores, axis=0, keepdims=True)) * (SCALE * LOG2E))
-                weights = (powers * (1.0 / jnp.sum(powers, axis=0, keepdims=True))).astype(BF16)
-                wsave[d, k, g] = weights
+                weights = softmax(d, l, k, d, g)
                 turned = weights.T
                 spreads.append(jnp.concatenate([turned * triangle[2], turned * triangle[3]], axis=1))
             for g in range(GROUP):
@@ -280,6 +327,14 @@
 
         lax.fori_loop(0, KV_HEADS, chunk, 0)
 
+    @pl.when(near_depth == 0)
+    def _():
+        normalize(near, 0, 0, near)
+
+    pl.semaphore_wait(barrier, count + 2)
+    for distance in range(1, count):
+        gain_copy(distance).start()
+
     def forward(v, carry):
         p = near_depth
         is_near = (v < p) | (v == 2 * p)
@@ -292,27 +347,121 @@
             pd = jnp.where(v == p, near, far)
             project(pd, jnp.where(v == p, near_depth, far_depth))
 
+            @pl.when((v == count) & (near_depth == 1))
+            def _():
+                for i in range(PIECES):
+                    quarter_copy(i).start()
+
         @pl.when(v == 0)
         def _():
             for distance in range(1, count):
                 gain_copy(distance).wait_recv()
+            make_masks()
 
         mix(d, l, depth)
         return carry
 
     lax.fori_loop(0, count + 1, forward, 0)
 
+    def prepare():
+        d = near
+
+        def pass_quarter(i, carry):
+            quarter_copy(i).wait_recv()
+            opposite_copy(i, side).start()
+            sibling_copy(i, 0, core).start()
+            return carry
+
+        def pass_opposite(i, carry):
+            opposite_copy(i, 1 - side).wait_recv()
+            sibling_copy(i, 1, core).start()
+            return carry
+
+        def take_sibling(i, carry):
+            sibling_copy(i, 0, 1 - core).wait_recv()
+            sibling_copy(i, 1, 1 - core).wait_recv()
+            return carry
+
+        for k in range(KV_HEADS):
+            back_copy(k).wait_recv()
+            s_copy(d, 1, k).start()
+        normalize(d, 1, 1, extra)
+
+        def chunk(k, carry):
+            s_copy(d, 1, k).wait_recv()
+            for g in range(GROUP):
+                softmax(d, 1, k, extra, g)
+            return carry
+
+        lax.fori_loop(0, KV_HEADS, chunk, 0)
+        lax.fori_loop(0, PIECES, pass_quarter, 0)
+        lax.fori_loop(0, PIECES, pass_opposite, 0)
+        lax.fori_loop(0, PIECES, take_sibling, 0)
+
     def backward(i, carry):
+        @pl.when((i != 1) | (near_depth == 0))
+        def _():
+            reverse_layer(i)
+
+        return carry
+
+    def reverse_layer(i):
+        repeated = i == 1
+        local = (i == 2) & (near_depth == 0)
         d = jnp.where(i == 0, far, near)
-        depth = jnp.where(i == 0, far_depth, near_depth)
+        depth = jnp.where(i == 0, far_depth, jnp.where(repeated, 1, near_depth))
+        slot = jnp.where(repeated, extra, d)
+        coming = jnp.where(local, 2, d)
+        leaving = jnp.where(repeated, 2, 3 + d)
+        first = depth == count - 1
+        streamed = (depth < count - 1) & ((i != 2) | (near_depth > 0))
         parity = lax.rem(depth, 2)
+        step = 2 * HEAD_DIM
+
+        @pl.when(repeated)
+        def _():
+            prepare()
+
+        def settle(k):
+            d_copy(slot, k).wait_recv()
+            for part in range(2):
+                total = downs[k, part].astype(F32) + drecv[slot, k, part].astype(F32)
+                dtot[slot, k, :, part * HEAD_DIM:(part + 1) * HEAD_DIM] = total.astype(BF16)
+
+                @pl.when(i != 1)
+                def _():
+                    kvg_copy(d, k, part).start()
+
+        def grad_part(k, t, u):
+            start = pl.multiple_of(t * tile + u * step, step)
+            return dot(dtot[slot, k], wbuf[slot, k, pl.ds(start, step), :], ((1,), (1,)))
+
+        def finish(k):
+            settle(k)
+
+            def part_tile(t, tile_carry):
+                for u in range(tile // step):
+                    cols = slice(u * step, (u + 1) * step)
+                    part = grad_part(k, t, u)
+                    gnbuf[t, :, cols] = jnp.where(k == 0, part, part + gnbuf[t, :, cols])
+                return tile_carry
+
+            lax.fori_loop(0, KV_HEADS, part_tile, 0)
 
         def chunk(k, inner_carry):
-            @pl.when(depth < count - 1)
-            def _():
-                c_copy(d, k).wait_recv()
-
-            @pl.when(depth == count - 1)
+            @pl.when((k > 0) & streamed)
+            def _():
+                finish(k - 1)
+
+            @pl.when(streamed)
+            def _():
+                c_copy(d, k, d).wait_recv()
+
+                @pl.when((depth == 1) & (i != 1))
+                def _():
+                    c_copy(d, k, d).start()
+
+            @pl.when(first)
             def _():
                 pltpu.make_async_copy(cbuf.at[d, k], cbuf.at[d, k], c_sem.at[d, k]).wait()
 
@@ -324,9 +473,9 @@
             )
             for g in range(GROUP):
                 cols = slice(g * HEAD_DIM, (g + 1) * HEAD_DIM)
-                cot = cbuf[d, k, :, cols]
+                cot = cbuf[coming, k, :, cols]
                 both = dot(values, cot, ((1,), (1,)))
-                weights = wsave[d, k, g]
+                weights = wsave[slot, k, g]
                 wide = weights.astype(F32)
                 grad_w = jnp.where(own_first, both[rows:], both[:rows]) * wide
                 mean = jnp.sum(grad_w, axis=0, keepdims=True)
@@ -335,7 +484,7 @@
                 own_s.append(grad_s * triangle[1])
                 earlier_w.append(weights * triangle[0])
                 own_w.append(weights * triangle[1])
-                queries.append(nbuf[d, k, :, cols])
+                queries.append(nbuf[slot, k, :, cols])
                 cots.append(cot)
                 turned = grad_s.T
                 spreads.append(jnp.concatenate([turned * triangle[2], turned * triangle[3]], axis=1))
@@ -350,36 +499,29 @@
             )
             grad_k = dot(all_s, jnp.concatenate(queries, axis=0), ((1,), (0,)))
             grad_v = dot(all_w, jnp.concatenate(cots, axis=0), ((1,), (0,)))
-            dsend[d, k, 0] = grad_k[:rows].astype(BF16)
-            dsend[d, k, 1] = grad_v[:rows].astype(BF16)
+            dsend[slot, k, 0] = grad_k[:rows].astype(BF16)
+            dsend[slot, k, 1] = grad_v[:rows].astype(BF16)
             downs[k, 0] = grad_k[rows:].astype(BF16)
             downs[k, 1] = grad_v[rows:].astype(BF16)
-            d_copy(d, k).start()
+            d_copy(slot, k).start()
+
+            @pl.when((k > 0) & ((i == 2) & (near_depth == 0) | first))
+            def _():
+                finish(k - 1)
+
             return inner_carry
 
         lax.fori_loop(0, KV_HEADS, chunk, 0)
-
-        for k in range(KV_HEADS):
-            d_copy(d, k).wait_recv()
-            for part in range(2):
-                total = downs[k, part].astype(F32) + drecv[d, k, part].astype(F32)
-                dtot[d, k, :, part * HEAD_DIM:(part + 1) * HEAD_DIM] = total.astype(BF16)
-                kvg_copy(d, k, part).start()
-
-        home = section
-        rstd = rstd_buf[d]
+        settle(KV_HEADS - 1)
+        home = depth + d * (count - 1 - 2 * depth)
+        rstd = rstd_buf[slot]
 
         def grad_tile(t, inner):
-            pairs = jnp.concatenate([dtot[d, k] for k in range(KV_HEADS)], axis=1)
-            step = 2 * HEAD_DIM
             for u in range(tile // step):
-                start = pl.multiple_of(t * tile + u * step, step)
-                weights = jnp.concatenate(
-                    [wbuf[d, k, pl.ds(start, step), :] for k in range(KV_HEADS)], axis=1
-                )
                 cols = slice(u * step, (u + 1) * step)
-                gain = gain_of(home, d, pl.ds(start, step))
-                grad_n = (dot(pairs, weights, ((1,), (1,))) + dqbuf[t, :, cols].astype(F32)) * gain
+                gain = gain_of(home, d, pl.ds(pl.multiple_of(t * tile + u * step, step), step))
+                grad = grad_part(KV_HEADS - 1, t, u) + gnbuf[t, :, cols]
+                grad_n = (grad + dqbuf[t, :, cols].astype(F32)) * gain
                 gnbuf[t, :, cols] = grad_n
                 product = grad_n * hbuf[d, parity, t, :, cols].astype(F32)
                 inner = inner + product[:, :HEAD_DIM] + product[:, HEAD_DIM:]
@@ -393,22 +535,42 @@
             for g in range(GROUP):
                 cols = slice(g * HEAD_DIM, (g + 1) * HEAD_DIM)
                 grad_h = gnbuf[t, :, cols] * rstd - hbuf[d, parity, t, :, cols].astype(F32) * factor
-                outc[d, t, :, cols] = (cbuf[d, t, :, cols].astype(F32) + grad_h).astype(BF16)
-
-            @pl.when(depth > 0)
-            def _():
-                c_copy(d, t).start()
-
-            ing_copy(d, t).start()
+                cbuf[leaving, t, :, cols] = (cbuf[coming, t, :, cols].astype(F32) + grad_h).astype(BF16)
+
+            @pl.when(depth > 1)
+            def _():
+                c_copy(d, t, 3 + d).start()
+
+            @pl.when(i != 1)
+            def _():
+                ing_copy(d, t).start()
+
             return inner_carry
 
         lax.fori_loop(0, KV_HEADS, total_tile, 0)
-        return carry
-
-    lax.fori_loop(0, 2, backward, 0)
+
+    lax.fori_loop(0, 3, backward, 0)
 
     for distance in range(1, count):
         gain_copy(distance).wait_send()
+
+    @pl.when(near_depth == 1)
+    def _():
+        for k in range(KV_HEADS):
+            back_copy(k).wait_send()
+        for i in range(PIECES):
+            quarter_copy(i).wait_send()
+
+    @pl.when(near_depth == 0)
+    def _():
+        for k in range(KV_HEADS):
+            s_copy(near, 1, k).wait_send()
+            d_copy(extra, k).wait_send()
+        for i in range(PIECES):
+            opposite_copy(i, side).wait_send()
+            sibling_copy(i, 0, core).wait_send()
+            sibling_copy(i, 1, core).wait_send()
+
     for d in range(2):
         depth = depth_of(d)
 
@@ -427,7 +589,7 @@
 
             @pl.when(depth > 0)
             def _():
-                c_copy(d, k).wait_send()
+                c_copy(d, k, d).wait_send()
 
             act_copy(d, lax.rem(depth + 1, 2), k).wait()
             ing_copy(d, k).wait()
@@ -453,22 +615,21 @@
             jax.ShapeDtypeStruct((2, 1, rows, pair_width), BF16),
         ],
         scratch_shapes=[
-            pltpu.VMEM((2, KV_HEADS, width, 2 * HEAD_DIM), BF16),
+            pltpu.VMEM((3, KV_HEADS, width, 2 * HEAD_DIM), BF16),
             pltpu.VMEM((2, 2, KV_HEADS, rows, tile), BF16),
-            pltpu.VMEM((2, KV_HEADS, rows, tile), BF16),
+            pltpu.VMEM((3, KV_HEADS, rows, tile), BF16),
             pltpu.VMEM((2, count, KV_HEADS, 2, 2 * rows, HEAD_DIM), BF16),
-            pltpu.VMEM((2, KV_HEADS, GROUP, rows, rows), BF16),
-            pltpu.VMEM((2, KV_HEADS, rows, tile), BF16),
-            pltpu.VMEM((2, KV_HEADS, rows, tile), BF16),
+            pltpu.VMEM((3, KV_HEADS, GROUP, rows, rows), BF16),
+            pltpu.VMEM((5, KV_HEADS, rows, tile), BF16),
             pltpu.VMEM((KV_HEADS, rows, tile), BF16),
             pltpu.VMEM((KV_HEADS, rows, tile), F32),
             pltpu.VMEM((count, 2, width), F32),
             pltpu.VMEM((2, 2 * rows, rows), F32),
-            pltpu.VMEM((2, rows, HEAD_DIM), F32),
-            pltpu.VMEM((2, KV_HEADS, 2, rows, HEAD_DIM), BF16),
-            pltpu.VMEM((2, KV_HEADS, 2, rows, HEAD_DIM), BF16),
+            pltpu.VMEM((3, rows, HEAD_DIM), F32),
+            pltpu.VMEM((3, KV_HEADS, 2, rows, HEAD_DIM), BF16),
+            pltpu.VMEM((3, KV_HEADS, 2, rows, HEAD_DIM), BF16),
             pltpu.VMEM((KV_HEADS, 2, rows, HEAD_DIM), BF16),
-            pltpu.VMEM((2, KV_HEADS, rows, 2 * HEAD_DIM), BF16),
+            pltpu.VMEM((3, KV_HEADS, rows, 2 * HEAD_DIM), BF16),
             pltpu.VMEM((4, rows, rows), BF16),
             pltpu.VMEM((2, rows, HEAD_DIM), F32),
             dma((2, KV_HEADS)),
@@ -483,11 +644,18 @@
             dma((2, count, KV_HEADS)),
             dma((2, KV_HEADS)),
             dma((2, KV_HEADS)),
-            dma((2, KV_HEADS)),
-            dma((2, KV_HEADS)),
+            dma((3, KV_HEADS)),
+            dma((3, KV_HEADS)),
             dma((2, KV_HEADS)),
             dma((2, KV_HEADS)),
             dma((2, KV_HEADS, 2)),
+            dma((KV_HEADS,)),
+            dma((PIECES,)),
+            dma((PIECES,)),
+            dma((PIECES,)),
+            dma((PIECES,)),
+            dma((2, PIECES)),
+            dma((2, PIECES)),
         ],
         compiler_params=pltpu.CompilerParams(
             collective_id=0, has_side_effects=True, vmem_limit_bytes=60 * 1024 * 1024

time: 165 us -> 160 us (0.970)
  Pallas kernels: 158 us -> 154 us
    pallas_call x1, Pallas kernels: 158 us -> 154 us  [per_device(): pl.pallas_call(functools.partial(relay_kernel, count, shards), in_specs=[...]
where the time goes in v3:
time: 160 us
  Pallas kernels  154 us (96%)
  local copies, waits for them, and re-layouts  5.47 us (3%)
    pallas_call x1, Pallas kernels, per_device(): pl.pallas_call(functools.partial(relay_kernel, count, shards), in_specs=[...  154 us
    unnamed x7, local copies, waits for them, and re-layouts  5.47 us

profile of v3, /device:TPU:1, one launch (start us, length us, event | category | flops | bytes accessed | tf_op | source)
XLA Modules:
  0.0 160.3 jit_solution(2222397786286802086)
XLA Ops:
  0.6 154.2 %relay.1 = (bf16[2,1,128,4096]{3,2,1,0:T(8,128)(2,1)}, bf16[2,1,128,4096]{3,2,1,0:T(8,128)(2,1)}, bf16[2,1,128,1024]{3,2,1,0:T(8,128)(2,1)}) custom-call(s32[2,16]{1,0:T(2,128)} %lengths_ref.1, bf16[128,4096]{1,0:T(8,128)(2,1)} %xa_ref.1, bf16[128,4096]{1,0:T(8,128)(2,1)} %xb_ref.1, bf16[128,4096]{1,0:T(8,128)(2,1)} %ga_ref.1, bf16[128,4096]{1,0:T(8,128)(2,1)} %gb_ref.1, ...), custom_call_target="tpu_custom_call" | custom-call | tf_op jit(solution)/shard_map/relay/pallas_call | solution.py:608
  154.8 0.0 copy-start
  154.8 3.3 %copy.13 = bf16[2,1,128,4096]{3,2,1,0:T(8,128)(2,1)} copy(bf16[2,1,128,4096]{3,2,1,0:T(8,128)(2,1)} %get-tuple-element.6) | data formatting | bytes 4194304
  158.1 0.0 copy-done
  158.1 0.0 copy-start.1
  158.1 1.3 copy.14
  159.4 0.1 copy-done.1
  159.5 0.8 copy.15
Async XLA Ops:
  154.8 3.3 %copy-start = (bf16[2,1,128,4096]{3,2,1,0:T(8,128)(2,1)S(1)}, bf16[2,1,128,4096]{3,2,1,0:T(8,128)(2,1)}, u32[]{:S(2)}) copy-start(bf16[2,1,128,4096]{3,2,1,0:T(8,128)(2,1)} %get-tuple-element.7) | copy-start | bytes 6291460
  158.1 1.4 copy-start.1

commit v4 on v3

--- a/solution.py
+++ b/solution.py
@@ -175,15 +175,8 @@
         x_copy(1, t).start()
     own_gain = pltpu.make_async_copy(gains_ref.at[0], gbuf.at[section], g_sem)
     own_gain.start()
-    for d in (near, far):
-        for k in range(KV_HEADS):
-            for part in range(2):
-                weight_copy(d, k, part).start()
-    for d, last in ((0, count - 1), (1, 0)):
-        @pl.when(section == last)
-        def _():
-            for t in range(KV_HEADS):
-                grad_copy(d, t).start()
+    for part in range(2):
+        weight_copy(near, 0, part).start()
 
     barrier = pltpu.get_barrier_semaphore()
     for neighbour in (following, preceding, opposite):
@@ -198,6 +191,15 @@
         x_copy(0, t).wait()
         x_copy(1, t).wait()
     own_gain.wait()
+    for d, start in ((near, 1), (far, 0)):
+        for k in range(start, KV_HEADS):
+            for part in range(2):
+                weight_copy(d, k, part).start()
+    for d, last in ((0, count - 1), (1, 0)):
+        @pl.when(section == last)
+        def _():
+            for t in range(KV_HEADS):
+                grad_copy(d, t).start()
 
     def gain_of(home, d, cols):
         return jnp.where(d == 0, gbuf[home, 0:1, cols], gbuf[home, 1:2, cols])
@@ -244,6 +246,16 @@
         triangle[2] = jnp.where(lane > sublane, 1.0, 0.0).astype(BF16)
         triangle[3] = jnp.where(lane <= sublane, 1.0, 0.0).astype(BF16)
 
+    middle = (near_depth == far_depth - 1) & (near_depth > 0)
+
+    def arrive(d, l, depth, k):
+        z_copy(d, l, k).wait_recv()
+        s_copy(d, l, k).start()
+
+        @pl.when(depth < count - 1)
+        def _():
+            z_copy(d, l, k).start()
+
     def project(d, depth):
         @pl.when(depth > 0)
         def _():
@@ -261,11 +273,13 @@
             def _():
                 z_copy(d, depth, k).start()
 
-            s_copy(d, depth, k).start()
-
-            @pl.when(depth == 1)
-            def _():
-                back_copy(k).start()
+            @pl.when(jnp.logical_not(middle & (depth == near_depth)))
+            def _():
+                s_copy(d, depth, k).start()
+
+            @pl.when(middle & (depth == near_depth))
+            def _():
+                arrive(far, 0, far_depth, k)
 
             return carry
 
@@ -284,27 +298,22 @@
 
         @pl.when(l < depth)
         def _():
+            home = l + d * (count - 1 - 2 * l)
+            gain_copy(lax.rem(section - home + count, count)).wait_recv()
             normalize(d, l, parity, d)
 
         squares_buf[d] = jnp.zeros((rows, HEAD_DIM), F32)
 
-        def arrive(k):
-            @pl.when(l < depth)
-            def _():
-                z_copy(d, l, k).wait_recv()
-
-                @pl.when(depth < count - 1)
-                def _():
-                    z_copy(d, l, k).start()
-
-                s_copy(d, l, k).start()
-
-        arrive(0)
+        coming = (l < depth) & ((l > 0) | (d == near) | jnp.logical_not(middle))
+
+        @pl.when(coming)
+        def _():
+            arrive(d, l, depth, 0)
 
         def chunk(k, carry):
-            @pl.when(k + 1 < KV_HEADS)
-            def _():
-                arrive(k + 1)
+            @pl.when((k + 1 < KV_HEADS) & coming)
+            def _():
+                arrive(d, l, depth, k + 1)
 
             s_copy(d, l, k).wait_recv()
             values = kv[d, l, k, 1]
@@ -337,31 +346,78 @@
 
     def forward(v, carry):
         p = near_depth
-        is_near = (v < p) | (v == 2 * p)
+        is_near = (v < p) | (v == jnp.where(p == 0, 0, count))
         d = jnp.where(is_near, near, far)
         depth = jnp.where(is_near, near_depth, far_depth)
-        l = jnp.where(v < p, v, jnp.where(v < 2 * p, v - p, jnp.where(v == 2 * p, p, v - p - 1)))
-
-        @pl.when((v == p) | (v == count))
+        l = jnp.where(is_near, jnp.where(v < p, v, p), jnp.where(p == 0, v - 1, v - p))
+        far_turn = jnp.where(p == 0, count, count - 1)
+
+        @pl.when((v == p) | (v == far_turn))
         def _():
             pd = jnp.where(v == p, near, far)
             project(pd, jnp.where(v == p, near_depth, far_depth))
 
-            @pl.when((v == count) & (near_depth == 1))
-            def _():
+            @pl.when((v == far_turn) & middle)
+            def _():
+                for k in range(KV_HEADS):
+                    s_copy(near, near_depth, k).start()
+
+            @pl.when((v == far_turn) & (near_depth == 1))
+            def _():
+                for k in range(KV_HEADS):
+                    back_copy(k).start()
                 for i in range(PIECES):
                     quarter_copy(i).start()
 
         @pl.when(v == 0)
         def _():
-            for distance in range(1, count):
-                gain_copy(distance).wait_recv()
             make_masks()
 
         mix(d, l, depth)
         return carry
 
     lax.fori_loop(0, count + 1, forward, 0)
+
+    def drain_forward():
+        for distance in range(1, count):
+            gain_copy(distance).wait_send()
+        for d in range(2):
+            depth = depth_of(d)
+
+            def layer_drain(l, carry):
+                for k in range(KV_HEADS):
+                    @pl.when(depth < count - 1)
+                    def _():
+                        z_copy(d, l, k).wait_send()
+
+                    s_copy(d, l, k).wait_send()
+                return carry
+
+            lax.fori_loop(0, depth + 1, layer_drain, 0)
+            for k in range(KV_HEADS):
+                act_copy(d, lax.rem(depth + 1, 2), k).wait()
+
+    def drain_reverse(d, depth):
+        for k in range(KV_HEADS):
+            d_copy(d, k).wait_send()
+
+            @pl.when(depth > 0)
+            def _():
+                c_copy(d, k, d).wait_send()
+
+            ing_copy(d, k).wait()
+            kvg_copy(d, k, 0).wait()
+            kvg_copy(d, k, 1).wait()
+
+    def pass_opposite(i, carry):
+        opposite_copy(i, 1 - side).wait_recv()
+        sibling_copy(i, 1, core).start()
+        return carry
+
+    def take_sibling(i, carry):
+        sibling_copy(i, 0, 1 - core).wait_recv()
+        sibling_copy(i, 1, 1 - core).wait_recv()
+        return carry
 
     def prepare():
         d = near
@@ -372,16 +428,6 @@
             sibling_copy(i, 0, core).start()
             return carry
 
-        def pass_opposite(i, carry):
-            opposite_copy(i, 1 - side).wait_recv()
-            sibling_copy(i, 1, core).start()
-            return carry
-
-        def take_sibling(i, carry):
-            sibling_copy(i, 0, 1 - core).wait_recv()
-            sibling_copy(i, 1, 1 - core).wait_recv()
-            return carry
-
         for k in range(KV_HEADS):
             back_copy(k).wait_recv()
             s_copy(d, 1, k).start()
@@ -395,8 +441,8 @@
 
         lax.fori_loop(0, KV_HEADS, chunk, 0)
         lax.fori_loop(0, PIECES, pass_quarter, 0)
-        lax.fori_loop(0, PIECES, pass_opposite, 0)
-        lax.fori_loop(0, PIECES, take_sibling, 0)
+        drain_forward()
+        drain_reverse(far, far_depth)
 
     def backward(i, carry):
         @pl.when((i != 1) | (near_depth == 0))
@@ -415,6 +461,7 @@
         leaving = jnp.where(repeated, 2, 3 + d)
         first = depth == count - 1
         streamed = (depth < count - 1) & ((i != 2) | (near_depth > 0))
+        added = streamed & (i != 1)
         parity = lax.rem(depth, 2)
         step = 2 * HEAD_DIM
 
@@ -449,7 +496,7 @@
             lax.fori_loop(0, KV_HEADS, part_tile, 0)
 
         def chunk(k, inner_carry):
-            @pl.when((k > 0) & streamed)
+            @pl.when((k > 0) & added)
             def _():
                 finish(k - 1)
 
@@ -505,13 +552,38 @@
             downs[k, 1] = grad_v[rows:].astype(BF16)
             d_copy(slot, k).start()
 
-            @pl.when((k > 0) & ((i == 2) & (near_depth == 0) | first))
-            def _():
-                finish(k - 1)
+            @pl.when(repeated & (k > 0) & (k < 3))
+            def _():
+                lax.fori_loop((k - 1) * (PIECES // 2), k * (PIECES // 2), pass_opposite, 0)
 
             return inner_carry
 
         lax.fori_loop(0, KV_HEADS, chunk, 0)
+
+        @pl.when(repeated)
+        def _():
+            lax.fori_loop(0, PIECES, take_sibling, 0)
+
+        @pl.when(jnp.logical_not(added))
+        def _():
+            for heads in (range(2), range(2, KV_HEADS - 1)):
+                for k in heads:
+                    settle(k)
+
+                def base_tile(t, tile_carry):
+                    for u in range(tile // step):
+                        start = pl.multiple_of(t * tile + u * step, step)
+                        cols = slice(u * step, (u + 1) * step)
+                        pairs = jnp.concatenate([dtot[slot, k] for k in heads], axis=1)
+                        weights = jnp.concatenate(
+                            [wbuf[slot, k, pl.ds(start, step), :] for k in heads], axis=1
+                        )
+                        part = dot(pairs, weights, ((1,), (1,)))
+                        gnbuf[t, :, cols] = part if heads[0] == 0 else part + gnbuf[t, :, cols]
+                    return tile_carry
+
+                lax.fori_loop(0, KV_HEADS, base_tile, 0)
+
         settle(KV_HEADS - 1)
         home = depth + d * (count - 1 - 2 * depth)
         rstd = rstd_buf[slot]
@@ -551,9 +623,6 @@
 
     lax.fori_loop(0, 3, backward, 0)
 
-    for distance in range(1, count):
-        gain_copy(distance).wait_send()
-
     @pl.when(near_depth == 1)
     def _():
         for k in range(KV_HEADS):
@@ -571,30 +640,12 @@
             sibling_copy(i, 0, core).wait_send()
             sibling_copy(i, 1, core).wait_send()
 
-    for d in range(2):
-        depth = depth_of(d)
-
-        def layer_drain(l, carry):
-            for k in range(KV_HEADS):
-                @pl.when(depth < count - 1)
-                def _():
-                    z_copy(d, l, k).wait_send()
-
-                s_copy(d, l, k).wait_send()
-            return carry
-
-        lax.fori_loop(0, depth + 1, layer_drain, 0)
-        for k in range(KV_HEADS):
-            d_copy(d, k).wait_send()
-
-            @pl.when(depth > 0)
-            def _():
-                c_copy(d, k, d).wait_send()
-
-            act_copy(d, lax.rem(depth + 1, 2), k).wait()
-            ing_copy(d, k).wait()
-            kvg_copy(d, k, 0).wait()
-            kvg_copy(d, k, 1).wait()
+    @pl.when(near_depth > 0)
+    def _():
+        drain_forward()
+        drain_reverse(far, far_depth)
+
+    drain_reverse(near, near_depth)
 
 
 def per_device(x_a, x_b, grad_a, grad_b, gains, kv_weights, doc_lengths):

time: 160 us -> 145 us (0.906)
  Pallas kernels: 154 us -> 139 us
    pallas_call x1, Pallas kernels: 154 us -> 139 us  [per_device(): pl.pallas_call(functools.partial(relay_kernel, count, shards), in_specs=[...]
where the time goes in v4:
time: 145 us
  Pallas kernels  139 us (96%)
  local copies, waits for them, and re-layouts  5.47 us (4%)
    pallas_call x1, Pallas kernels, per_device(): pl.pallas_call(functools.partial(relay_kernel, count, shards), in_specs=[...  139 us
    unnamed x7, local copies, waits for them, and re-layouts  5.47 us

profile of v4, /device:TPU:1, one launch (start us, length us, event | category | flops | bytes accessed | tf_op | source)
XLA Modules:
  0.0 145.0 jit_solution(2560913118792872168)
XLA Ops:
  0.6 138.9 %relay.1 = (bf16[2,1,128,4096]{3,2,1,0:T(8,128)(2,1)}, bf16[2,1,128,4096]{3,2,1,0:T(8,128)(2,1)}, bf16[2,1,128,1024]{3,2,1,0:T(8,128)(2,1)}) custom-call(s32[2,16]{1,0:T(2,128)} %lengths_ref.1, bf16[128,4096]{1,0:T(8,128)(2,1)} %xa_ref.1, bf16[128,4096]{1,0:T(8,128)(2,1)} %xb_ref.1, bf16[128,4096]{1,0:T(8,128)(2,1)} %ga_ref.1, bf16[128,4096]{1,0:T(8,128)(2,1)} %gb_ref.1, ...), custom_call_target="tpu_custom_call" | custom-call | tf_op jit(solution)/shard_map/relay/pallas_call | solution.py:659
  139.5 0.0 copy-start
  139.5 3.3 %copy.13 = bf16[2,1,128,4096]{3,2,1,0:T(8,128)(2,1)} copy(bf16[2,1,128,4096]{3,2,1,0:T(8,128)(2,1)} %get-tuple-element.6) | data formatting | bytes 4194304
  142.8 0.0 copy-done
  142.8 0.0 copy-start.1
  142.8 1.3 copy.14
  144.1 0.1 copy-done.1
  144.2 0.8 copy.15
Async XLA Ops:
  139.5 3.3 %copy-start = (bf16[2,1,128,4096]{3,2,1,0:T(8,128)(2,1)S(1)}, bf16[2,1,128,4096]{3,2,1,0:T(8,128)(2,1)}, u32[]{:S(2)}) copy-start(bf16[2,1,128,4096]{3,2,1,0:T(8,128)(2,1)} %get-tuple-element.7) | copy-start | bytes 6291460
  142.8 1.4 copy-start.1

commit v5 on v4

--- a/solution.py
+++ b/solution.py
@@ -104,10 +104,11 @@
             device_id={"seq": following}, device_id_type=MESH,
         )
 
-    def c_copy(d, t, slot):
-        return pltpu.make_async_remote_copy(
-            src_ref=cbuf.at[slot, t], dst_ref=cbuf.at[d, t],
-            send_sem=cs_sem.at[d, t], recv_sem=cr_sem.at[d, t],
+    def c_copy(d, t, slot, part):
+        lines = pl.ds(part * (rows // 2), rows // 2)
+        return pltpu.make_async_remote_copy(
+            src_ref=cbuf.at[slot, t, lines, :], dst_ref=cbuf.at[d, t, lines, :],
+            send_sem=cs_sem.at[d, t, part], recv_sem=cr_sem.at[d, t, part],
             device_id={"section": section - 1 + 2 * d}, device_id_type=MESH,
         )
 
@@ -304,7 +305,8 @@
 
         squares_buf[d] = jnp.zeros((rows, HEAD_DIM), F32)
 
-        coming = (l < depth) & ((l > 0) | (d == near) | jnp.logical_not(middle))
+        coming = (l < depth) & ((d == near) | ((l == 0) & jnp.logical_not(middle)))
+        ahead = (d == far) & (l + 1 < far_depth)
 
         @pl.when(coming)
         def _():
@@ -332,6 +334,10 @@
             def _():
                 act_copy(d, 1 - parity, k).start()
 
+            @pl.when(ahead)
+            def _():
+                arrive(far, l + 1, far_depth, k)
+
             return carry
 
         lax.fori_loop(0, KV_HEADS, chunk, 0)
@@ -341,8 +347,8 @@
         normalize(near, 0, 0, near)
 
     pl.semaphore_wait(barrier, count + 2)
-    for distance in range(1, count):
-        gain_copy(distance).start()
+    closest = lax.rem(1 - 2 * near + count, count)
+    gain_copy(closest).start()
 
     def forward(v, carry):
         p = near_depth
@@ -371,6 +377,8 @@
 
         @pl.when(v == 0)
         def _():
+            for further in range(1, count - 1):
+                gain_copy(1 + lax.rem(closest - 1 + further, count - 1)).start()
             make_masks()
 
         mix(d, l, depth)
@@ -403,7 +411,8 @@
 
             @pl.when(depth > 0)
             def _():
-                c_copy(d, k, d).wait_send()
+                for part in range(2):
+                    c_copy(d, k, d, part).wait_send()
 
             ing_copy(d, k).wait()
             kvg_copy(d, k, 0).wait()
@@ -496,17 +505,14 @@
             lax.fori_loop(0, KV_HEADS, part_tile, 0)
 
         def chunk(k, inner_carry):
-            @pl.when((k > 0) & added)
-            def _():
-                finish(k - 1)
-
             @pl.when(streamed)
             def _():
-                c_copy(d, k, d).wait_recv()
-
-                @pl.when((depth == 1) & (i != 1))
-                def _():
-                    c_copy(d, k, d).start()
+                for part in range(2):
+                    c_copy(d, k, d, part).wait_recv()
+
+                    @pl.when((depth == 1) & (i != 1))
+                    def _():
+                        c_copy(d, k, d, part).start()
 
             @pl.when(first)
             def _():
@@ -552,6 +558,10 @@
             downs[k, 1] = grad_v[rows:].astype(BF16)
             d_copy(slot, k).start()
 
+            @pl.when((k > 0) & added)
+            def _():
+                finish(k - 1)
+
             @pl.when(repeated & (k > 0) & (k < 3))
             def _():
                 lax.fori_loop((k - 1) * (PIECES // 2), k * (PIECES // 2), pass_opposite, 0)
@@ -611,7 +621,8 @@
 
             @pl.when(depth > 1)
             def _():
-                c_copy(d, t, 3 + d).start()
+                for part in range(2):
+                    c_copy(d, t, 3 + d, part).start()
 
             @pl.when(i != 1)
             def _():
@@ -648,6 +659,45 @@
     drain_reverse(near, near_depth)
 
 
+def hand_over_kernel(acts_ref, ingrad_ref, kvgrad_ref, acts_out, ingrad_out, kvgrad_out, wide, narrow, in_sem, out_sem):
+    lines = acts_ref.shape[2] // 2
+    moves = []
+    for d in range(2):
+        for part in range(2):
+            block = (d, 0, pl.ds(part * lines, lines))
+            for a, (source, target) in enumerate(((acts_ref, acts_out), (ingrad_ref, ingrad_out))):
+                moves.append((source.at[block], wide.at[a, d, part], target.at[block]))
+        moves.append((kvgrad_ref.at[d, 0], narrow.at[d], kvgrad_out.at[d, 0]))
+    inward = [pltpu.make_async_copy(m[0], m[1], in_sem.at[i]) for i, m in enumerate(moves)]
+    outward = [pltpu.make_async_copy(m[1], m[2], out_sem.at[i]) for i, m in enumerate(moves)]
+    for copy in inward:
+        copy.start()
+    for taken, given in zip(inward, outward):
+        taken.wait()
+        given.start()
+    for copy in outward:
+        copy.wait()
+
+
+def hand_over(acts, ingrads, kvgrads):
+    rows, width = acts.shape[2:]
+    anywhere = pl.BlockSpec(memory_space=pl.ANY)
+    return pl.pallas_call(
+        hand_over_kernel,
+        in_specs=[anywhere] * 3,
+        out_specs=[anywhere] * 3,
+        out_shape=[jax.ShapeDtypeStruct(a.shape, a.dtype) for a in (acts, ingrads, kvgrads)],
+        scratch_shapes=[
+            pltpu.VMEM((2, 2, 2, rows // 2, width), BF16),
+            pltpu.VMEM((2, rows, kvgrads.shape[3]), BF16),
+            pltpu.SemaphoreType.DMA((10,)),
+            pltpu.SemaphoreType.DMA((10,)),
+        ],
+        compiler_params=pltpu.CompilerParams(vmem_limit_bytes=60 * 1024 * 1024),
+        name="hand_over",
+    )(acts, ingrads, kvgrads)
+
+
 def per_device(x_a, x_b, grad_a, grad_b, gains, kv_weights, doc_lengths):
     count = lax.axis_size("section")
     shards = lax.axis_size("seq")
@@ -656,7 +706,7 @@
     tile = width // KV_HEADS
     dma = pltpu.SemaphoreType.DMA
     anywhere = pl.BlockSpec(memory_space=pl.ANY)
-    return pl.pallas_call(
+    results = pl.pallas_call(
         functools.partial(relay_kernel, count, shards),
         in_specs=[pl.BlockSpec(memory_space=pltpu.SMEM)] + [anywhere] * 6,
         out_specs=[anywhere] * 3,
@@ -693,8 +743,8 @@
             dma((2, count, KV_HEADS)),
             dma((2, count, KV_HEADS)),
             dma((2, count, KV_HEADS)),
-            dma((2, KV_HEADS)),
-            dma((2, KV_HEADS)),
+            dma((2, KV_HEADS, 2)),
+            dma((2, KV_HEADS, 2)),
             dma((3, KV_HEADS)),
             dma((3, KV_HEADS)),
             dma((2, KV_HEADS)),
@@ -713,6 +763,7 @@
         ),
         name="relay",
     )(doc_lengths, x_a, x_b, grad_a, grad_b, gains, kv_weights)
+    return hand_over(*results)
 
 
 def solution(mesh):

time: 145 us -> 137 us (0.945)
  local copies, waits for them, and re-layouts: 5.47 us -> 0 us
  Pallas kernels: 139 us -> 136 us
    pallas_call x1, Pallas kernels: 139 us -> 132 us  [per_device(): pl.pallas_call(functools.partial(relay_kernel, count, shards), in_specs=[...]
    unnamed x7 -> x0, local copies, waits for them, and re-layouts: 5.47 us -> none
    pallas_call x0 -> x1, Pallas kernels: none -> 4.07 us  [hand_over(): pl.pallas_call(hand_over_kernel, in_specs=[anywhere] * 3, out_specs=[anyw...]
where the time goes in v5:
time: 137 us
  Pallas kernels  136 us (99%)
    pallas_call x1, Pallas kernels, per_device(): pl.pallas_call(functools.partial(relay_kernel, count, shards), in_specs=[...  132 us
    pallas_call x1, Pallas kernels, hand_over(): pl.pallas_call(hand_over_kernel, in_specs=[anywhere] * 3, out_specs=[anyw...  4.07 us

profile of v5, /device:TPU:1, one launch (start us, length us, event | category | flops | bytes accessed | tf_op | source)
XLA Modules:
  0.0 137.1 jit_solution(1985718866905362905)
XLA Ops:
  0.6 132.4 %relay.1 = (bf16[2,1,128,4096]{3,2,1,0:T(8,128)(2,1)}, bf16[2,1,128,4096]{3,2,1,0:T(8,128)(2,1)}, bf16[2,1,128,1024]{3,2,1,0:T(8,128)(2,1)}) custom-call(s32[2,16]{1,0:T(2,128)} %lengths_ref.1, bf16[128,4096]{1,0:T(8,128)(2,1)} %xa_ref.1, bf16[128,4096]{1,0:T(8,128)(2,1)} %xb_ref.1, bf16[128,4096]{1,0:T(8,128)(2,1)} %ga_ref.1, bf16[128,4096]{1,0:T(8,128)(2,1)} %gb_ref.1, ...), custom_call_target="tpu_custom_call" | custom-call | tf_op jit(solution)/shard_map/relay/pallas_call | solution.py:709
  133.0 4.1 %hand_over.1 = (bf16[2,1,128,4096]{3,2,1,0:T(8,128)(2,1)}, bf16[2,1,128,4096]{3,2,1,0:T(8,128)(2,1)}, bf16[2,1,128,1024]{3,2,1,0:T(8,128)(2,1)}) custom-call(bf16[2,1,128,4096]{3,2,1,0:T(8,128)(2,1)} %get-tuple-element.6.acts_ref, bf16[2,1,128,4096]{3,2,1,0:T(8,128)(2,1)} %get-tuple-element.7.ingrad_ref, bf16[2,1,128,1024]{3,2,1,0:T(8,128)(2,1)} %get-tuple-element.8.kvgrad_ref), custom_call_target="tpu_custom_call" | custom-call | tf_op jit(solution)/shard_map/hand_over/pallas_call | solution.py:685

commit v6 on v5

--- a/solution.py
+++ b/solution.py
@@ -15,6 +15,7 @@
 SCALE = 1.0 / math.sqrt(HEAD_DIM)
 LOG2E = math.log2(math.e)
 PIECES = 8
+PARTS = 4
 
 epsilon = 1e-05
 
@@ -32,7 +33,7 @@
     lengths_ref, xa_ref, xb_ref, ga_ref, gb_ref, gains_ref, weights_ref,
     acts_ref, ingrad_ref, kvgrad_ref,
     wbuf, hbuf, nbuf, kv, wsave, cbuf, dqbuf, gnbuf, gbuf, bias, rstd_buf,
-    dsend, drecv, downs, dtot, triangle, squares_buf,
+    dsend, drecv, downs, dtot, triangle, squares_buf, inner_buf,
     x_sem, w_sem, c_sem, g_sem, gs_sem, gr_sem,
     zs_sem, zr_sem, ss_sem, sr_sem, cs_sem, cr_sem, ds_sem, dr_sem,
     act_sem, ing_sem, kvg_sem,
@@ -105,7 +106,7 @@
         )
 
     def c_copy(d, t, slot, part):
-        lines = pl.ds(part * (rows // 2), rows // 2)
+        lines = pl.ds(part * (rows // PARTS), rows // PARTS)
         return pltpu.make_async_remote_copy(
             src_ref=cbuf.at[slot, t, lines, :], dst_ref=cbuf.at[d, t, lines, :],
             send_sem=cs_sem.at[d, t, part], recv_sem=cr_sem.at[d, t, part],
@@ -310,13 +311,10 @@
 
         @pl.when(coming)
         def _():
-            arrive(d, l, depth, 0)
+            for k in range(KV_HEADS):
+                arrive(d, l, depth, k)
 
         def chunk(k, carry):
-            @pl.when((k + 1 < KV_HEADS) & coming)
-            def _():
-                arrive(d, l, depth, k + 1)
-
             s_copy(d, l, k).wait_recv()
             values = kv[d, l, k, 1]
             spreads = []
@@ -411,7 +409,7 @@
 
             @pl.when(depth > 0)
             def _():
-                for part in range(2):
+                for part in range(PARTS):
                     c_copy(d, k, d, part).wait_send()
 
             ing_copy(d, k).wait()
@@ -507,7 +505,7 @@
         def chunk(k, inner_carry):
             @pl.when(streamed)
             def _():
-                for part in range(2):
+                for part in range(PARTS):
                     c_copy(d, k, d, part).wait_recv()
 
                     @pl.when((depth == 1) & (i != 1))
@@ -576,40 +574,35 @@
 
         @pl.when(jnp.logical_not(added))
         def _():
-            for heads in (range(2), range(2, KV_HEADS - 1)):
-                for k in heads:
-                    settle(k)
-
-                def base_tile(t, tile_carry):
-                    for u in range(tile // step):
-                        start = pl.multiple_of(t * tile + u * step, step)
-                        cols = slice(u * step, (u + 1) * step)
-                        pairs = jnp.concatenate([dtot[slot, k] for k in heads], axis=1)
-                        weights = jnp.concatenate(
-                            [wbuf[slot, k, pl.ds(start, step), :] for k in heads], axis=1
-                        )
-                        part = dot(pairs, weights, ((1,), (1,)))
-                        gnbuf[t, :, cols] = part if heads[0] == 0 else part + gnbuf[t, :, cols]
-                    return tile_carry
-
-                lax.fori_loop(0, KV_HEADS, base_tile, 0)
+            for k in range(KV_HEADS - 1):
+                settle(k)
 
         settle(KV_HEADS - 1)
         home = depth + d * (count - 1 - 2 * depth)
         rstd = rstd_buf[slot]
-
-        def grad_tile(t, inner):
+        inner_buf[...] = jnp.zeros((rows, HEAD_DIM), F32)
+
+        def grad_tile(heads, t, tile_carry):
             for u in range(tile // step):
                 cols = slice(u * step, (u + 1) * step)
-                gain = gain_of(home, d, pl.ds(pl.multiple_of(t * tile + u * step, step), step))
-                grad = grad_part(KV_HEADS - 1, t, u) + gnbuf[t, :, cols]
-                grad_n = (grad + dqbuf[t, :, cols].astype(F32)) * gain
+                start = pl.multiple_of(t * tile + u * step, step)
+                pairs = jnp.concatenate([dtot[slot, k] for k in heads], axis=1)
+                weights = jnp.concatenate([wbuf[slot, k, pl.ds(start, step), :] for k in heads], axis=1)
+                grad = dot(pairs, weights, ((1,), (1,)))
+                if len(heads) < KV_HEADS:
+                    grad = grad + gnbuf[t, :, cols]
+                grad_n = (grad + dqbuf[t, :, cols].astype(F32)) * gain_of(home, d, pl.ds(start, step))
                 gnbuf[t, :, cols] = grad_n
                 product = grad_n * hbuf[d, parity, t, :, cols].astype(F32)
-                inner = inner + product[:, :HEAD_DIM] + product[:, HEAD_DIM:]
-            return inner
-
-        inner = lax.fori_loop(0, KV_HEADS, grad_tile, jnp.zeros((rows, HEAD_DIM), F32))
+                inner_buf[...] += product[:, :HEAD_DIM] + product[:, HEAD_DIM:]
+            return tile_carry
+
+        for whole, heads in ((False, range(KV_HEADS - 1, KV_HEADS)), (True, range(KV_HEADS))):
+            @pl.when(added != whole)
+            def _():
+                lax.fori_loop(0, KV_HEADS, functools.partial(grad_tile, heads), 0)
+
+        inner = inner_buf[...]
         inner = jnp.broadcast_to(jnp.sum(inner, axis=-1, keepdims=True), (rows, HEAD_DIM))
         factor = inner * (1.0 / width) * rstd * rstd * rstd
 
@@ -621,7 +614,7 @@
 
             @pl.when(depth > 1)
             def _():
-                for part in range(2):
+                for part in range(PARTS):
                     c_copy(d, t, 3 + d, part).start()
 
             @pl.when(i != 1)
@@ -733,6 +726,7 @@
             pltpu.VMEM((3, KV_HEADS, rows, 2 * HEAD_DIM), BF16),
             pltpu.VMEM((4, rows, rows), BF16),
             pltpu.VMEM((2, rows, HEAD_DIM), F32),
+            pltpu.VMEM((rows, HEAD_DIM), F32),
             dma((2, KV_HEADS)),
             dma((2, KV_HEADS, 2)),
             dma((2, KV_HEADS)),
@@ -743,8 +737,8 @@
             dma((2, count, KV_HEADS)),
             dma((2, count, KV_HEADS)),
             dma((2, count, KV_HEADS)),
-            dma((2, KV_HEADS, 2)),
-            dma((2, KV_HEADS, 2)),
+            dma((2, KV_HEADS, PARTS)),
+            dma((2, KV_HEADS, PARTS)),
             dma((3, KV_HEADS)),
             dma((3, KV_HEADS)),
             dma((2, KV_HEADS)),

time: 137 us -> 137 us (level); the launches traced: 137 us -> 135 us
    pallas_call x1, Pallas kernels: 132 us -> 131 us  [per_device(): pl.pallas_call(functools.partial(relay_kernel, count, shards), in_specs=[...]
where the time goes in v6:
time: 137 us; the launch traced here: 135 us
  Pallas kernels  135 us (99%)
    pallas_call x1, Pallas kernels, per_device(): pl.pallas_call(functools.partial(relay_kernel, count, shards), in_specs=[...  131 us
    pallas_call x1, Pallas kernels, hand_over(): pl.pallas_call(hand_over_kernel, in_specs=[anywhere] * 3, out_specs=[anyw...  4.07 us

profile of v6, /device:TPU:1, one launch (start us, length us, event | category | flops | bytes accessed | tf_op | source)
XLA Modules:
  0.0 135.4 jit_solution(5179380702802524594)
XLA Ops:
  0.6 130.7 %relay.1 = (bf16[2,1,128,4096]{3,2,1,0:T(8,128)(2,1)}, bf16[2,1,128,4096]{3,2,1,0:T(8,128)(2,1)}, bf16[2,1,128,1024]{3,2,1,0:T(8,128)(2,1)}) custom-call(s32[2,16]{1,0:T(2,128)} %lengths_ref.1, bf16[128,4096]{1,0:T(8,128)(2,1)} %xa_ref.1, bf16[128,4096]{1,0:T(8,128)(2,1)} %xb_ref.1, bf16[128,4096]{1,0:T(8,128)(2,1)} %ga_ref.1, bf16[128,4096]{1,0:T(8,128)(2,1)} %gb_ref.1, ...), custom_call_target="tpu_custom_call" | custom-call | tf_op jit(solution)/shard_map/relay/pallas_call | solution.py:702
  131.3 4.1 %hand_over.1 = (bf16[2,1,128,4096]{3,2,1,0:T(8,128)(2,1)}, bf16[2,1,128,4096]{3,2,1,0:T(8,128)(2,1)}, bf16[2,1,128,1024]{3,2,1,0:T(8,128)(2,1)}) custom-call(bf16[2,1,128,4096]{3,2,1,0:T(8,128)(2,1)} %get-tuple-element.6.acts_ref, bf16[2,1,128,4096]{3,2,1,0:T(8,128)(2,1)} %get-tuple-element.7.ingrad_ref, bf16[2,1,128,1024]{3,2,1,0:T(8,128)(2,1)} %get-tuple-element.8.kvgrad_ref), custom_call_target="tpu_custom_call" | custom-call | tf_op jit(solution)/shard_map/hand_over/pallas_call | solution.py:678

commit v7 on v6

--- a/solution.py
+++ b/solution.py
@@ -264,6 +264,10 @@
             normalize(d, depth, lax.rem(depth, 2), d)
 
         def chunk(k, carry):
+            @pl.when(middle & (depth == near_depth))
+            def _():
+                arrive(far, 0, far_depth, k)
+
             weight_copy(d, k, 0).wait()
             weight_copy(d, k, 1).wait()
             normed = jnp.concatenate([nbuf[d, t] for t in range(KV_HEADS)], axis=1)
@@ -278,10 +282,6 @@
             @pl.when(jnp.logical_not(middle & (depth == near_depth)))
             def _():
                 s_copy(d, depth, k).start()
-
-            @pl.when(middle & (depth == near_depth))
-            def _():
-                arrive(far, 0, far_depth, k)
 
             return carry
 

time: 137 us -> 136 us (level)
  no operation moved by 1% of the time
where the time goes in v7:
time: 136 us; the launch traced here: 135 us
  Pallas kernels  134 us (99%)
    pallas_call x1, Pallas kernels, per_device(): pl.pallas_call(functools.partial(relay_kernel, count, shards), in_specs=[...  130 us
    pallas_call x1, Pallas kernels, hand_over(): pl.pallas_call(hand_over_kernel, in_specs=[anywhere] * 3, out_specs=[anyw...  4.07 us

profile of v7, /device:TPU:1, one launch (start us, length us, event | category | flops | bytes accessed | tf_op | source)
XLA Modules:
  0.0 134.7 jit_solution(11025980450216312745)
XLA Ops:
  0.6 130.0 %relay.1 = (bf16[2,1,128,4096]{3,2,1,0:T(8,128)(2,1)}, bf16[2,1,128,4096]{3,2,1,0:T(8,128)(2,1)}, bf16[2,1,128,1024]{3,2,1,0:T(8,128)(2,1)}) custom-call(s32[2,16]{1,0:T(2,128)} %lengths_ref.1, bf16[128,4096]{1,0:T(8,128)(2,1)} %xa_ref.1, bf16[128,4096]{1,0:T(8,128)(2,1)} %xb_ref.1, bf16[128,4096]{1,0:T(8,128)(2,1)} %ga_ref.1, bf16[128,4096]{1,0:T(8,128)(2,1)} %gb_ref.1, ...), custom_call_target="tpu_custom_call" | custom-call | tf_op jit(solution)/shard_map/relay/pallas_call | solution.py:702
  130.7 4.1 %hand_over.1 = (bf16[2,1,128,4096]{3,2,1,0:T(8,128)(2,1)}, bf16[2,1,128,4096]{3,2,1,0:T(8,128)(2,1)}, bf16[2,1,128,1024]{3,2,1,0:T(8,128)(2,1)}) custom-call(bf16[2,1,128,4096]{3,2,1,0:T(8,128)(2,1)} %get-tuple-element.6.acts_ref, bf16[2,1,128,4096]{3,2,1,0:T(8,128)(2,1)} %get-tuple-element.7.ingrad_ref, bf16[2,1,128,1024]{3,2,1,0:T(8,128)(2,1)} %get-tuple-element.8.kvgrad_ref), custom_call_target="tpu_custom_call" | custom-call | tf_op jit(solution)/shard_map/hand_over/pallas_call | solution.py:678

commit v8 on v7

--- a/solution.py
+++ b/solution.py
@@ -172,6 +172,15 @@
             kvg_sem.at[d, k, part],
         )
 
+    barrier = pltpu.get_barrier_semaphore()
+    for neighbour in (following, preceding, opposite):
+        pl.semaphore_signal(barrier, inc=1, device_id={"seq": neighbour}, device_id_type=MESH)
+    for distance in range(1, count):
+        pl.semaphore_signal(
+            barrier, inc=1, device_id={"section": lax.rem(section + distance, count)},
+            device_id_type=MESH,
+        )
+
     for t in range(KV_HEADS):
         x_copy(0, t).start()
         x_copy(1, t).start()
@@ -179,15 +188,6 @@
     own_gain.start()
     for part in range(2):
         weight_copy(near, 0, part).start()
-
-    barrier = pltpu.get_barrier_semaphore()
-    for neighbour in (following, preceding, opposite):
-        pl.semaphore_signal(barrier, inc=1, device_id={"seq": neighbour}, device_id_type=MESH)
-    for distance in range(1, count):
-        pl.semaphore_signal(
-            barrier, inc=1, device_id={"section": lax.rem(section + distance, count)},
-            device_id_type=MESH,
-        )
 
     for t in range(KV_HEADS):
         x_copy(0, t).wait()

time: 136 us -> 136 us (level)
  no operation moved by 1% of the time
where the time goes in v8:
time: 136 us; the launch traced here: 135 us
  Pallas kernels  134 us (99%)
    pallas_call x1, Pallas kernels, per_device(): pl.pallas_call(functools.partial(relay_kernel, count, shards), in_specs=[...  130 us
    pallas_call x1, Pallas kernels, hand_over(): pl.pallas_call(hand_over_kernel, in_specs=[anywhere] * 3, out_specs=[anyw...  4.07 us

profile of v8, /device:TPU:1, one launch (start us, length us, event | category | flops | bytes accessed | tf_op | source)
XLA Modules:
  0.0 135.0 jit_solution(5511304701870203879)
XLA Ops:
  0.6 130.2 %relay.1 = (bf16[2,1,128,4096]{3,2,1,0:T(8,128)(2,1)}, bf16[2,1,128,4096]{3,2,1,0:T(8,128)(2,1)}, bf16[2,1,128,1024]{3,2,1,0:T(8,128)(2,1)}) custom-call(s32[2,16]{1,0:T(2,128)} %lengths_ref.1, bf16[128,4096]{1,0:T(8,128)(2,1)} %xa_ref.1, bf16[128,4096]{1,0:T(8,128)(2,1)} %xb_ref.1, bf16[128,4096]{1,0:T(8,128)(2,1)} %ga_ref.1, bf16[128,4096]{1,0:T(8,128)(2,1)} %gb_ref.1, ...), custom_call_target="tpu_custom_call" | custom-call | tf_op jit(solution)/shard_map/relay/pallas_call | solution.py:702
  130.9 4.1 %hand_over.1 = (bf16[2,1,128,4096]{3,2,1,0:T(8,128)(2,1)}, bf16[2,1,128,4096]{3,2,1,0:T(8,128)(2,1)}, bf16[2,1,128,1024]{3,2,1,0:T(8,128)(2,1)}) custom-call(bf16[2,1,128,4096]{3,2,1,0:T(8,128)(2,1)} %get-tuple-element.6.acts_ref, bf16[2,1,128,4096]{3,2,1,0:T(8,128)(2,1)} %get-tuple-element.7.ingrad_ref, bf16[2,1,128,1024]{3,2,1,0:T(8,128)(2,1)} %get-tuple-element.8.kvgrad_ref), custom_call_target="tpu_custom_call" | custom-call | tf_op jit(solution)/shard_map/hand_over/pallas_call | solution.py:678
